TPU v7x, 32 devices: a whole 2x2x4 slice. The times are simulated.
32 devices in a mesh: dp: 16 (over z, x, core), seq: 2 (over y).
Axes of the slice: x: 2, y: 2, z: 4, core: 2. Of those that a mesh axis runs over, the one named last changes fastest.
Arguments:
- y_one: bfloat16 [16, 392, 576], P('dp', 'seq'), may hold values from -6 to 6
- second_stream: bfloat16 [16, 392, 576], P('dp', 'seq'), may hold values from -6 to 6
- d_one: bfloat16 [16, 392, 576], P('dp', 'seq'), may hold values from -6 to 6
- d_two: bfloat16 [16, 392, 576], P('dp', 'seq'), may hold values from -6 to 6
- layer_norm_gain: float32 [576], replicated, may hold values from 0.1 to 1.9
- w_qkv: bfloat16 [576, 1728], P('dp'), may hold values from -1 to 1
- w_out: bfloat16 [576, 576], P('dp'), may hold values from -0.25 to 0.25
- frames_valid: int32 [16], P('dp'), may hold values from 1 to 2, as said below
Outputs:
- x_one: bfloat16 [16, 392, 576], P('dp', 'seq')
- dx_two: bfloat16 [16, 392, 576], P('dp', 'seq')
- grad_qkv: float32 [576, 1728], P('dp', 'seq')
Inputs may be any that keep to these rules, and one draw needn't show every extreme that they name: `frames_valid`: frames of a clip at or beyond its count are padding; some clip has all 2 frames and some clip has 1.
All inputs are finite; a program needn't handle non-finite values.
Results may differ from a plain program's by a relative error of at most 0.018.
The roundings to bfloat16 on the way count: a program that leaves them out, or rounds other values in their place, can miss the bound.
Values may be sent and summed in bfloat16 or wider, within the bound.
No kernel may reach another device: no remote copies, remote signals or barrier semaphores. Data moves between devices by JAX's collectives and lax.ppermute only.
A program may use at most 64 MiB of HBM per device.

v0:
```python
import functools
import math

import jax
import jax.numpy as jnp
from jax import lax
from jax.experimental import pallas as pl
from jax.experimental.pallas import tpu as pltpu
from jax.sharding import PartitionSpec as P

HEADS = 8
SIDE = 14
POOL = 2
PSIDE = 7
FRAME_TOK = 196
PFRAME = 49


def pool_table():
    token_ids = jnp.arange(FRAME_TOK, dtype=jnp.int32)
    pooled_ids = jnp.arange(PFRAME, dtype=jnp.int32)
    token_row = token_ids // SIDE // POOL
    token_col = token_ids % SIDE // POOL
    hits = (
        (token_row[None, :] == (pooled_ids // PSIDE)[:, None])
        & (token_col[None, :] == (pooled_ids % PSIDE)[:, None])
    ).astype(jnp.float32)
    return hits / jnp.sum(hits, axis=1, keepdims=True)


def normalize_rows(inputs):
    values = inputs.astype(jnp.float32)
    centered = values - jnp.mean(values, axis=-1, keepdims=True)
    inverse_deviation = lax.rsqrt(jnp.mean(centered * centered, axis=-1, keepdims=True) + 1e-05)
    return (centered * inverse_deviation, inverse_deviation)


def pool_rows(table, rows):
    frame_count = rows.shape[0] // FRAME_TOK
    shaped = rows.reshape(frame_count, FRAME_TOK, rows.shape[1])
    pooled = jnp.einsum("pt,ftw->fpw", table, shaped, precision=lax.Precision.HIGHEST)
    return pooled.reshape(frame_count * PFRAME, rows.shape[1])


def spread_rows(table, pooled):
    frame_count = pooled.shape[0] // PFRAME
    shaped = pooled.reshape(frame_count, PFRAME, pooled.shape[1])
    spread = jnp.einsum("pt,fpw->ftw", table, shaped, precision=lax.Precision.HIGHEST)
    return spread.reshape(frame_count * FRAME_TOK, pooled.shape[1])


def masked_softmax(scores, key_live):
    masked = jnp.where(key_live[None, None, :], scores, -jnp.inf)
    top = jnp.max(masked, axis=-1, keepdims=True)
    raised = jnp.exp(masked - top)
    return raised / jnp.sum(raised, axis=-1, keepdims=True)


def local_general(y_one, second_stream, d_one, d_two, layer_norm_gain, w_qkv, w_out, frames_valid):
    seq_count = lax.axis_size("seq")
    clip_count = lax.axis_size("dp")
    model_width = w_out.shape[1]
    tokens_here = second_stream.shape[1]
    head_width = model_width // HEADS
    full_qkv, full_out = (
        lax.all_gather(w_qkv, "dp", axis=0, tiled=True),
        lax.all_gather(w_out, "dp", axis=0, tiled=True),
    )
    table = pool_table()
    scale = 1.0 / math.sqrt(head_width)
    grad_scale = 1.0 / math.sqrt(clip_count * seq_count * tokens_here)
    upper = y_one[0]
    cot_one = d_one[0]
    standardized_input, inverse_deviation = normalize_rows(second_stream[0])
    normed_rows = (standardized_input * layer_norm_gain).astype(jnp.bfloat16)
    projected = jnp.dot(normed_rows, full_qkv, preferred_element_type=jnp.float32)
    queries = projected[:, :model_width].astype(jnp.bfloat16)
    own_pooled = pool_rows(table, projected[:, model_width:]).astype(jnp.bfloat16)
    all_pooled = lax.all_gather(own_pooled, "seq", axis=0, tiled=True)
    key_total = all_pooled.shape[0]
    key_live = jnp.arange(key_total, dtype=jnp.int32) // PFRAME < frames_valid[0]
    query_heads = queries.reshape(tokens_here, HEADS, head_width)
    key_heads = all_pooled[:, :model_width].reshape(key_total, HEADS, head_width)
    value_heads = all_pooled[:, model_width:].reshape(key_total, HEADS, head_width)
    scores = (
        jnp.einsum("nhe,mhe->hnm", query_heads, key_heads, preferred_element_type=jnp.float32)
        * scale
    )
    probs = masked_softmax(scores, key_live).astype(jnp.bfloat16)
    mixed_wide = jnp.einsum("hnm,mhe->nhe", probs, value_heads, preferred_element_type=jnp.float32)
    mixed = mixed_wide.reshape(tokens_here, model_width).astype(jnp.bfloat16)
    branch = jnp.dot(mixed, full_out, preferred_element_type=jnp.float32)
    x_one = (upper.astype(jnp.float32) - branch).astype(jnp.bfloat16)
    d_mixed = lax.dot_general(
        cot_one, full_out, (((1,), (1,)), ((), ())), preferred_element_type=jnp.float32
    ).astype(jnp.bfloat16)
    d_heads = d_mixed.reshape(tokens_here, HEADS, head_width)
    d_probs = jnp.einsum("nhe,mhe->hnm", d_heads, value_heads, preferred_element_type=jnp.float32)
    delta = jnp.einsum("nhe,nhe->hn", d_heads.astype(jnp.float32), mixed_wide)
    d_scores = (probs.astype(jnp.float32) * (d_probs - delta[:, :, None]) * scale).astype(
        jnp.bfloat16
    )
    d_queries = (
        jnp.einsum("hnm,mhe->nhe", d_scores, key_heads, preferred_element_type=jnp.float32)
        .reshape(tokens_here, model_width)
        .astype(jnp.bfloat16)
    )
    key_term = jnp.einsum(
        "hnm,nhe->mhe", d_scores, query_heads, preferred_element_type=jnp.float32
    ).reshape(key_total, model_width)
    value_term = jnp.einsum(
        "hnm,nhe->mhe", probs, d_heads, preferred_element_type=jnp.float32
    ).reshape(key_total, model_width)
    own_grads = lax.psum_scatter(
        jnp.concatenate([key_term, value_term], axis=1).astype(jnp.bfloat16),
        "seq",
        scatter_dimension=0,
        tiled=True,
    ).astype(jnp.float32)
    d_tokens = spread_rows(table, own_grads).astype(jnp.bfloat16)
    d_projected = jnp.concatenate([d_queries, d_tokens], axis=1)
    d_normed = lax.dot_general(
        d_projected, full_qkv, (((1,), (1,)), ((), ())), preferred_element_type=jnp.float32
    )
    gain_applied = d_normed * layer_norm_gain
    lower_gradient = inverse_deviation * (
        gain_applied
        - jnp.mean(gain_applied, axis=-1, keepdims=True)
        - standardized_input * jnp.mean(gain_applied * standardized_input, axis=-1, keepdims=True)
    )
    dx_two = (d_two[0].astype(jnp.float32) + lower_gradient).astype(jnp.bfloat16)
    qkv_term = (
        lax.dot_general(
            normed_rows, d_projected, (((0,), (0,)), ((), ())), preferred_element_type=jnp.float32
        )
        * grad_scale
    )
    column_qkv = lax.psum_scatter(
        qkv_term.astype(jnp.bfloat16), "seq", scatter_dimension=1, tiled=True
    ).astype(jnp.float32)
    grad_qkv = lax.psum_scatter(column_qkv, "dp", scatter_dimension=0, tiled=True)
    return (x_one[None], dx_two[None], grad_qkv)


AXES = ("dp", "seq")
OVER_Y, OVER_CORE, OVER_X, OVER_Z1, OVER_Z2 = 1, 2, 4, 8, 16

D = 576
HALF = 288
HEAD = 72
HERE = 4
ROWS = 36
SLOT = 48
REL = 16 * SLOT
FSLOT = 208
TOK2 = 2 * FSLOT
KEYS = 128
KLANES = HERE * KEYS
QKV = 3 * HALF
SHARD = QKV + D
SEND = 640 + HALF
BF16, F32 = jnp.bfloat16, jnp.float32


def swap(array, mask):
    return lax.ppermute(array, AXES, [(i, i ^ mask) for i in range(32)])


def dot(a, b, dims=((1,), (0,))):
    return lax.dot_general(a, b, (dims, ((), ())), preferred_element_type=F32)


SLOTS = ("o", "x", "a", "xa", "b", "xb", "ab", "xab")
NT = ((1,), (1,))
TN = ((0,), (0,))


def iota(shape, dim):
    return lax.broadcasted_iota(jnp.int32, shape, dim)


def feature_of_slot(shape, dim):
    me = lax.axis_index("dp")
    at = iota(shape, dim)
    feature = jnp.full(shape, -1, jnp.int32)
    for s in range(16):
        rel = ((s & 7) << 1) | (s >> 3)
        here = (at >= SLOT * s) & (at < SLOT * s + ROWS)
        feature = jnp.where(here, (me ^ rel) * ROWS + at - SLOT * s, feature)
    return feature


def one_hot(hits):
    return jnp.where(hits, 1.0, 0.0).astype(BF16)


def key_of_token(shape, dim):
    at = iota(shape, dim)
    second = at >= FSLOT
    t = jnp.where(second, at - FSLOT, at)
    row = (t * 9363) >> 17
    col = t - row * SIDE
    key = (row >> 1) * PSIDE + (col >> 1) + jnp.where(second, 64, 0)
    return jnp.where(t < FRAME_TOK, key, -1)


def shard_kernel(qkv_hbm, out_hbm, own_ref, qkv_ref, out_ref, sems):
    loads = (
        pltpu.make_async_copy(qkv_hbm, qkv_ref, sems.at[0]),
        pltpu.make_async_copy(out_hbm, out_ref, sems.at[1]),
    )
    for load in loads:
        load.start()
    for load in loads:
        load.wait()
    y = lax.axis_index("seq")
    for s in range(2):

        @pl.when(y == s)
        def _():
            for part in range(3):
                at = part * D + s * HALF
                own_ref[:, part * HALF : (part + 1) * HALF] = qkv_ref[:, at : at + HALF]

    own_ref[:, QKV:] = out_ref[...]


def standardize(values):
    centered = values - jnp.mean(values, axis=-1, keepdims=True)
    inverse = lax.rsqrt(jnp.mean(centered * centered, axis=-1, keepdims=True) + 1e-05)
    return centered * inverse, inverse


def prep_kernel(own_ref, peer_ref, gain_ref, rel_ref, relt_ref, pool_ref, poolt_ref, order_ref):
    order = one_hot(iota((D, REL), 0) == feature_of_slot((1, REL), 1))
    order_t = one_hot(feature_of_slot((REL, 1), 0) == iota((REL, D), 1))
    order_ref[...] = order
    gain = gain_ref[...].reshape(1, D)
    for f, src in enumerate((own_ref, peer_ref)):
        normed = (standardize(src[...].astype(F32))[0] * gain).astype(BF16)
        normed = jnp.concatenate([normed, jnp.zeros((FSLOT - FRAME_TOK, D), BF16)], axis=0)
        rel_ref[f * FSLOT : (f + 1) * FSLOT, :] = dot(normed, order).astype(BF16)
        relt_ref[f] = dot(order_t, normed, NT).astype(BF16)
    table = one_hot(iota((KEYS, TOK2), 0) == key_of_token((1, TOK2), 1)) * BF16(0.25)
    pooled = dot(table, rel_ref[...])
    hi = pooled.astype(BF16)
    pool_ref[:KEYS, :] = hi
    pool_ref[KEYS:, :] = (pooled - hi.astype(F32)).astype(BF16)
    pooled_t = dot(relt_ref[0], table[:, :FSLOT], NT) + dot(relt_ref[1], table[:, FSLOT:], NT)
    hi_t = pooled_t.astype(BF16)
    poolt_ref[:, :KEYS] = hi_t
    poolt_ref[:, KEYS:] = (pooled_t - hi_t.astype(F32)).astype(BF16)


def head_lanes(h):
    lane = iota((1, HALF), 1)
    return (lane >= h * HEAD) & (lane < (h + 1) * HEAD)


def main_kernel(grad_scale, valid_ref, rel_ref, relt_ref, pool_ref, poolt_ref, order_ref, down_ref, dpeer_ref, *rest):
    blocks = rest[:16]
    gown_ref, goth_ref, w_ref, dq_ref, e_ref, mixed_ref, outh_ref = rest[16:23]
    cot_ref, kbig_ref, vbig_ref, s_ref, p_ref, ds_ref, g_ref = rest[23:]
    y = lax.axis_index("seq")
    scale = 1.0 / math.sqrt(HEAD)
    for s in range(16):
        w_ref[s * SLOT + 32 : (s + 1) * SLOT, :] = jnp.zeros((16, SHARD), BF16)
        w_ref[s * SLOT : s * SLOT + ROWS, :] = blocks[s][...]
    for f, src in enumerate((down_ref, dpeer_ref)):
        at = f * FSLOT
        cot_ref[at + 192 : at + FSLOT, :] = jnp.zeros((16, D), BF16)
        cot_ref[at : at + FRAME_TOK, :] = src[...]

    queries = dot(rel_ref[...], w_ref[:, :HALF]).astype(BF16)
    kv = dot(pool_ref[...], w_ref[:, 256:QKV])
    kv = kv[:KEYS] + kv[KEYS:]
    keys = kv[:, 32 : 32 + HALF].astype(BF16)
    values = kv[:, 32 + HALF :].astype(BF16)
    for h in range(HERE):
        lanes = head_lanes(h)
        kbig_ref[h * KEYS : (h + 1) * KEYS, :] = jnp.where(lanes, keys, BF16(0))
        vbig_ref[h * KEYS : (h + 1) * KEYS, :] = jnp.where(lanes, values, BF16(0))
    select = order_ref[pl.ds(pl.multiple_of(y * HALF, HALF), HALF), :]
    outh_ref[...] = dot(select, w_ref[:, QKV:]).astype(BF16)
    d_mixed = dot(cot_ref[...], outh_ref[...], NT).astype(BF16)

    s_ref[...] = dot(queries, kbig_ref[...], NT)
    key = iota((1, KEYS), 1)
    late = key >= 64
    frame = jnp.where(late, 1 - y, y)
    live = (jnp.where(late, key - 64, key) < PFRAME) & (frame < valid_ref[0])
    for h in range(HERE):
        cols = slice(h * KEYS, (h + 1) * KEYS)
        for f in range(2):
            rows = slice(f * FSLOT, (f + 1) * FSLOT)
            masked = jnp.where(live, s_ref[rows, cols] * scale, -jnp.inf)
            raised = jnp.exp(masked - jnp.max(masked, axis=-1, keepdims=True))
            p_ref[rows, cols] = (raised / jnp.sum(raised, axis=-1, keepdims=True)).astype(BF16)
    mixed_ref[...] = dot(p_ref[...], vbig_ref[...]).astype(BF16)
    s_ref[...] = dot(d_mixed, vbig_ref[...], NT)
    for h in range(HERE):
        cols = slice(h * KEYS, (h + 1) * KEYS)
        for f in range(2):
            rows = slice(f * FSLOT, (f + 1) * FSLOT)
            wide = p_ref[rows, cols].astype(F32)
            d_probs = s_ref[rows, cols]
            delta = jnp.sum(wide * d_probs, axis=-1, keepdims=True)
            ds_ref[rows, cols] = (wide * (d_probs - delta) * scale).astype(BF16)
    dq_ref[:, 256:384] = jnp.zeros((TOK2, 128), BF16)
    dq_ref[:, :HALF] = dot(ds_ref[...], kbig_ref[...]).astype(BF16)

    def by_head(big):
        return sum(jnp.where(head_lanes(h), big[h * KEYS : (h + 1) * KEYS], 0.0) for h in range(HERE))

    d_keys = by_head(dot(ds_ref[...], queries, TN)) * 0.25
    d_values = by_head(dot(p_ref[...], d_mixed, TN)) * 0.25
    e = jnp.concatenate([jnp.zeros((KEYS, 32), F32), d_keys, d_values], axis=1).astype(BF16)
    e_ref[:KEYS, :] = e
    e_ref[KEYS:, :] = e
    dq = dq_ref[...]
    g_q = dot(relt_ref[0], dq[:FSLOT]) + dot(relt_ref[1], dq[FSLOT:])
    g_kv = dot(poolt_ref[...], e_ref[...]) * 4.0
    g_ref[:, :256] = g_q[:, :256] * grad_scale
    g_ref[:, 256:384] = (g_q[:, 256:] + g_kv[:, :128]) * grad_scale
    g_ref[:, 384:] = g_kv[:, 128:] * grad_scale
    for s in range(8):
        gown_ref[s] = g_ref[s * SLOT : s * SLOT + ROWS, :].astype(BF16)
        goth_ref[s] = g_ref[(s + 8) * SLOT : (s + 8) * SLOT + ROWS, :].astype(BF16)


def cross_kernel(w_ref, dq_ref, e_ref, mixed_ref, order_ref, send_ref, dn_ref):
    spread = one_hot(key_of_token((TOK2, 1), 0) == iota((TOK2, KEYS), 1))
    d_tokens = dot(spread, e_ref[:KEYS, :]).astype(BF16)
    d_normed = dot(dq_ref[...], w_ref[:, :384], NT) + dot(d_tokens, w_ref[:, 256:QKV], NT)
    dn_ref[...] = d_normed[:FSLOT]
    peer = dot(d_normed[FSLOT:].astype(BF16), order_ref[...], NT)
    send_ref[:, :D] = peer[:FRAME_TOK].astype(BF16)
    send_ref[:, D:640] = jnp.zeros((FRAME_TOK, 640 - D), BF16)
    send_ref[:, 640:] = mixed_ref[FSLOT : FSLOT + FRAME_TOK, :]


def late_kernel(w_ref, dn_ref, order_ref, nat_ref, oth_ref):
    order = order_ref[...]
    hi = dn_ref[...].astype(BF16)
    lo = (dn_ref[...] - hi.astype(F32)).astype(BF16)
    nat_ref[...] = (dot(hi, order, NT) + dot(lo, order, NT))[:FRAME_TOK]
    other = 1 - lax.axis_index("seq")
    select = order_ref[pl.ds(pl.multiple_of(other * HALF, HALF), HALF), :]
    oth_ref[...] = dot(select, w_ref[:, QKV:]).astype(BF16)


def last_kernel(yone_ref, second_ref, dtwo_ref, gain_ref, got_ref, dn_ref, mixed_ref, outh_ref, oth_ref, x_ref, dx_ref):
    branch = dot(mixed_ref[:FRAME_TOK, :], outh_ref[...]) + dot(got_ref[:, 640:], oth_ref[...])
    x_ref[...] = (yone_ref[...].astype(F32) - branch).astype(BF16)
    xhat, inverse = standardize(second_ref[...].astype(F32))
    gained = (dn_ref[...] + got_ref[:, :D].astype(F32)) * gain_ref[...].reshape(1, D)
    lower = inverse * (
        gained
        - jnp.mean(gained, axis=-1, keepdims=True)
        - xhat * jnp.mean(gained * xhat, axis=-1, keepdims=True)
    )
    dx_ref[...] = (dtwo_ref[...].astype(F32) + lower).astype(BF16)


def split_kernel(own_ref, got_ref, *outs):
    for s in range(8):
        outs[s][...] = (own_ref[s].astype(F32) + got_ref[s].astype(F32)).astype(BF16)


def add_kernel(a_ref, b_ref, sum_ref):
    sum_ref[...] = (a_ref[...].astype(F32) + b_ref[...].astype(F32)).astype(BF16)


def sum_kernel(*refs):
    terms, (total_ref, cross_ref) = refs[:-2], refs[-2:]
    total = sum(t[...].astype(F32) for t in terms)
    total_ref[...] = total
    y = lax.axis_index("seq")

    @pl.when(y == 0)
    def _():
        cross_ref[...] = total[:, 2 * HALF :]

    @pl.when(y == 1)
    def _():
        cross_ref[...] = total[:, :HALF]


def join_kernel(total_ref, cross_ref, grad_ref):
    y = lax.axis_index("seq")
    grad_ref[:, HALF : 2 * HALF] = cross_ref[...]
    for s in range(2):

        @pl.when(y == s)
        def _():
            grad_ref[:, :HALF] = total_ref[:, s * HALF : (s + 1) * HALF]
            grad_ref[:, 2 * HALF :] = total_ref[:, (s + 1) * HALF : (s + 2) * HALF]


def shape(*dims, kind=BF16):
    return jax.ShapeDtypeStruct(dims, kind)


def call(kernel, outs, args, scratch=(), smem=0, hbm=False, flops=0, moved=0, limit=16):
    vmem = pl.BlockSpec(memory_space=pltpu.VMEM)
    source = pl.BlockSpec(memory_space=pltpu.HBM) if hbm else vmem
    return pl.pallas_call(
        kernel,
        out_shape=outs,
        in_specs=[pl.BlockSpec(memory_space=pltpu.SMEM)] * smem + [source] * (len(args) - smem),
        out_specs=jax.tree.map(lambda _: vmem, outs),
        scratch_shapes=scratch,
        compiler_params=pltpu.CompilerParams(vmem_limit_bytes=limit << 20),
        cost_estimate=pl.CostEstimate(flops=flops, bytes_accessed=moved, transcendentals=0),
    )(*args)


def paired_body(y_one, second_stream, d_one, d_two, layer_norm_gain, w_qkv, w_out, frames_valid):
    grad_scale = 1.0 / math.sqrt(lax.axis_size("dp") * 2 * FRAME_TOK)
    second, cot = second_stream[0], d_one[0]
    gain = layer_norm_gain

    own = call(
        shard_kernel,
        shape(ROWS, SHARD),
        (w_qkv, w_out),
        scratch=(
            pltpu.VMEM((ROWS, 2 * QKV), BF16),
            pltpu.VMEM((ROWS, D), BF16),
            pltpu.SemaphoreType.DMA((2,)),
        ),
        hbm=True,
        moved=400_000,
        limit=60,
    )
    by_b = swap(own, OVER_Z2)
    by_x = swap(own, OVER_X)
    by_a = swap(own, OVER_Z1)
    second_peer = swap(second, OVER_Y)
    cot_peer = swap(cot, OVER_Y)
    by_ab = swap(by_b, OVER_Z1)
    by_xb = swap(by_b, OVER_X)
    by_xa = swap(by_a, OVER_X)
    by_xab = swap(by_ab, OVER_X)
    mine = (own, by_x, by_a, by_xa, by_b, by_xb, by_ab, by_xab)
    other = tuple(swap(block, OVER_CORE) for block in mine)

    rel, rel_t, pool, pool_t, order = call(
        prep_kernel,
        (shape(TOK2, REL), shape(2, REL, FSLOT), shape(2 * KEYS, REL), shape(REL, 2 * KEYS), shape(D, REL)),
        (second, second_peer, gain),
        flops=1_200_000_000,
        moved=3_000_000,
    )
    g_own, g_oth, w_rel, d_q, e, mixed, out_own = call(
        functools.partial(main_kernel, grad_scale),
        (
            shape(8, ROWS, QKV),
            shape(8, ROWS, QKV),
            shape(REL, SHARD),
            shape(TOK2, 384),
            shape(2 * KEYS, 608),
            shape(TOK2, HALF),
            shape(HALF, D),
        ),
        (frames_valid, rel, rel_t, pool, pool_t, order, cot, cot_peer) + mine + other,
        scratch=(
            pltpu.VMEM((TOK2, D), BF16),
            pltpu.VMEM((KLANES, HALF), BF16),
            pltpu.VMEM((KLANES, HALF), BF16),
            pltpu.VMEM((TOK2, KLANES), F32),
            pltpu.VMEM((TOK2, KLANES), BF16),
            pltpu.VMEM((TOK2, KLANES), BF16),
            pltpu.VMEM((REL, QKV), F32),
        ),
        smem=1,
        flops=4_000_000_000,
        moved=8_000_000,
        limit=32,
    )

    block = shape(ROWS, QKV)

    def add(a, b):
        return call(add_kernel, block, (a, b), moved=200_000)

    chunk = call(split_kernel, (block,) * 8, (g_own, swap(g_oth, OVER_CORE)), moved=1_500_000)
    by_slot = dict(zip(SLOTS, chunk))
    terms = [by_slot["o"], swap(by_slot["x"], OVER_X)]
    for name, mask in (("ab", OVER_Z1 | OVER_Z2), ("b", OVER_Z2), ("a", OVER_Z1)):
        summed = add(by_slot[name], swap(by_slot["x" + name], OVER_X))
        terms.append(swap(summed, mask))
    total, crossing = call(
        sum_kernel,
        (shape(ROWS, QKV, kind=F32), shape(ROWS, HALF, kind=F32)),
        tuple(terms),
        moved=500_000,
    )
    crossed = swap(crossing, OVER_Y)
    grad_qkv = call(join_kernel, shape(ROWS, QKV, kind=F32), (total, crossed), moved=300_000)

    send, d_normed = call(
        cross_kernel,
        (shape(FRAME_TOK, SEND), shape(FSLOT, REL, kind=F32)),
        (w_rel, d_q, e, mixed, order),
        flops=1_200_000_000,
        moved=4_000_000,
    )
    got = swap(send, OVER_Y)
    d_normed, out_oth = call(
        late_kernel,
        (shape(FRAME_TOK, D, kind=F32), shape(HALF, D)),
        (w_rel, d_normed, order),
        flops=600_000_000,
        moved=3_000_000,
    )
    x_one, dx_two = call(
        last_kernel,
        (shape(FRAME_TOK, D), shape(FRAME_TOK, D)),
        (y_one[0], second, d_two[0], gain, got, d_normed, mixed, out_own, out_oth),
        flops=300_000_000,
        moved=3_000_000,
    )
    return (x_one[None], dx_two[None], grad_qkv)


def local_paired(*args):
    return paired_body(*args)


def solution(mesh):
    in_specs = (
        P("dp", "seq", None),
        P("dp", "seq", None),
        P("dp", "seq", None),
        P("dp", "seq", None),
        P(),
        P("dp", None),
        P("dp", None),
        P("dp"),
    )
    out_specs = (P("dp", "seq", None), P("dp", "seq", None), P("dp", "seq"))
    paired = dict(mesh.shape) == {"dp": 16, "seq": 2}
    local = local_paired if paired else local_general
    return jax.shard_map(local, mesh=mesh, in_specs=in_specs, out_specs=out_specs, check_vma=False)
```

profile of v0, /device:TPU:0, one launch (start us, length us, event | category | flops | bytes accessed | tf_op | source)
XLA Modules:
  0.0 58.9 jit_solution(18277440970844535211)
XLA Ops:
  0.6 1.8 %shard_map.104.rest_0_ = bf16[36,1440]{1,0:T(8,128)(2,1)} custom-call(bf16[36,1728]{1,0:T(8,128)(2,1)} %qkv_hbm.1, bf16[36,576]{1,0:T(8,128)(2,1)} %out_hbm.1), custom_call_target="tpu_custom_call" | custom-call | bytes 400000 | tf_op jit(solution)/shard_map/pallas_call | solution.py:407
  2.4 4.1 %collective-permute-start.5 = (bf16[36,1440]{1,0:T(8,128)(2,1)}, bf16[36,1440]{1,0:T(8,128)(2,1)S(1)}, u32[]{:S(2)}, u32[]{:S(2)}) collective-permute-start(bf16[36,1440]{1,0:T(8,128)(2,1)} %shard_map.104.rest_0_), channel_id=1, source_target_pairs={{0,16},{1,17},{2,18},{3,19},{4,20},{5,21},{6,22},{7,23},{8,24},{9,... | collective-permute-start | bytes 311048 | tf_op jit(solution)/shard_map/ppermute | solution.py:166
  6.6 1.6 %collective-permute-start.3 = (bf16[36,1440]{1,0:T(8,128)(2,1)}, bf16[36,1440]{1,0:T(8,128)(2,1)S(1)}, u32[]{:S(2)}, u32[]{:S(2)}) collective-permute-start(bf16[36,1440]{1,0:T(8,128)(2,1)} %shard_map.104.rest_0_), channel_id=1, source_target_pairs={{0,8},{1,9},{2,10},{3,11},{4,12},{5,13},{6,14},{7,15},{8,0},{9,1},... | collective-permute-start | bytes 311048 | tf_op jit(solution)/shard_map/ppermute | solution.py:166
  8.2 1.5 %collective-permute-start.2 = (bf16[36,1440]{1,0:T(8,128)(2,1)}, bf16[36,1440]{1,0:T(8,128)(2,1)S(1)}, u32[]{:S(2)}, u32[]{:S(2)}) collective-permute-start(bf16[36,1440]{1,0:T(8,128)(2,1)} %shard_map.104.rest_0_), channel_id=1, source_target_pairs={{0,4},{1,5},{2,6},{3,7},{4,0},{5,1},{6,2},{7,3},{8,12},{9,13},{10,... | collective-permute-start | bytes 311048 | tf_op jit(solution)/shard_map/ppermute | solution.py:166
  9.6 1.5 %collective-permute-start = (bf16[196,576]{1,0:T(8,128)(2,1)}, bf16[196,576]{1,0:T(8,128)(2,1)S(1)}, u32[]{:S(2)}, u32[]{:S(2)}) collective-permute-start(bf16[196,576]{1,0:T(8,128)(2,1)} %bitcast.7), channel_id=1, source_target_pairs={{0,1},{1,0},{2,3},{3,2},{4,5},{5,4},{6,7},{7,6},{8,9},{9,8},{10,11... | collective-permute-start | bytes 677384 | tf_op jit(solution)/shard_map/ppermute | solution.py:166
  11.2 1.7 %collective-permute-done.5.rest_4_ = bf16[36,1440]{1,0:T(8,128)(2,1)S(1)} collective-permute-done((bf16[36,1440]{1,0:T(8,128)(2,1)}, bf16[36,1440]{1,0:T(8,128)(2,1)S(1)}, u32[]{:S(2)}, u32[]{:S(2)}) %collective-permute-start.5) | collective-permute-done | bytes 103712 | tf_op jit(solution)/shard_map/ppermute | solution.py:166
  14.0 1.5 %collective-permute-start.6 = (bf16[36,1440]{1,0:T(8,128)(2,1)S(1)}, bf16[36,1440]{1,0:T(8,128)(2,1)S(1)}, u32[]{:S(2)}, u32[]{:S(2)}) collective-permute-start(bf16[36,1440]{1,0:T(8,128)(2,1)S(1)} %collective-permute-done.5.rest_4_), channel_id=1, source_target_pairs={{0,4},{1,5},{2,6},{3,7},{4,0},{5,1},{6,2},{7,3},{8,12},{9,13},{10,... | collective-permute-start | bytes 311048 | tf_op jit(solution)/shard_map/ppermute | solution.py:166
  15.5 1.6 %collective-permute-start.1 = (bf16[196,576]{1,0:T(8,128)(2,1)}, bf16[196,576]{1,0:T(8,128)(2,1)S(1)}, u32[]{:S(2)}, u32[]{:S(2)}) collective-permute-start(bf16[196,576]{1,0:T(8,128)(2,1)} %bitcast.11), channel_id=1, source_target_pairs={{0,1},{1,0},{2,3},{3,2},{4,5},{5,4},{6,7},{7,6},{8,9},{9,8},{10,11... | collective-permute-start | bytes 677384 | tf_op jit(solution)/shard_map/ppermute | solution.py:166
  17.1 1.4 %collective-permute-done.7.rest_6_ = bf16[36,1440]{1,0:T(8,128)(2,1)S(1)} collective-permute-done((bf16[36,1440]{1,0:T(8,128)(2,1)S(1)}, bf16[36,1440]{1,0:T(8,128)(2,1)S(1)}, u32[]{:S(2)}, u32[]{:S(2)}) %collective-permute-start.7) | collective-permute-done | bytes 103712 | tf_op jit(solution)/shard_map/ppermute | solution.py:166
  18.6 1.5 %collective-permute-start.4 = (bf16[36,1440]{1,0:T(8,128)(2,1)S(1)}, bf16[36,1440]{1,0:T(8,128)(2,1)S(1)}, u32[]{:S(2)}, u32[]{:S(2)}) collective-permute-start(bf16[36,1440]{1,0:T(8,128)(2,1)S(1)} %collective-permute-done.3.rest_2_), channel_id=1, source_target_pairs={{0,4},{1,5},{2,6},{3,7},{4,0},{5,1},{6,2},{7,3},{8,12},{9,13},{10,... | collective-permute-start | bytes 311048 | tf_op jit(solution)/shard_map/ppermute | solution.py:166
  21.3 2.5 %collective-permute-done.4.rest_3_ = bf16[36,1440]{1,0:T(8,128)(2,1)S(1)} collective-permute-done((bf16[36,1440]{1,0:T(8,128)(2,1)S(1)}, bf16[36,1440]{1,0:T(8,128)(2,1)S(1)}, u32[]{:S(2)}, u32[]{:S(2)}) %collective-permute-start.4) | collective-permute-done | bytes 103712 | tf_op jit(solution)/shard_map/ppermute | solution.py:166
  24.4 1.7 %collective-permute-done.8.rest_7_ = bf16[36,1440]{1,0:T(8,128)(2,1)S(1)} collective-permute-done((bf16[36,1440]{1,0:T(8,128)(2,1)S(1)}, bf16[36,1440]{1,0:T(8,128)(2,1)S(1)}, u32[]{:S(2)}, u32[]{:S(2)}) %collective-permute-start.8) | collective-permute-done | bytes 103712 | tf_op jit(solution)/shard_map/ppermute | solution.py:166
  27.7 2.4 %shard_map.103 = (bf16[416,768]{1,0:T(8,128)(2,1)S(1)}, bf16[2,768,208]{2,1,0:T(8,128)(2,1)S(1)}, bf16[256,768]{1,0:T(8,128)(2,1)S(1)}, bf16[768,256]{1,0:T(8,128)(2,1)S(1)}, bf16[576,768]{1,0:T(8,128)(2,1)S(1)}) custom-call(bf16[196,576]{1,0:T(8,128)(2,1)S(1)} %bitcast.8, bf16[196,576]{1,0:T(8,128)(2,1)S(1)} %collective-permute-done.peer_ref, f32[576]{0:T(1024)S(1)} %copy-done.5), custom_call_target="tpu_custom_call" | custom-call | flops 1200000000 | bytes 3000000 | tf_op jit(solution)/shard_map/pallas_call | solution.py:407
  30.2 4.5 %shard_map.105 = (bf16[8,36,864]{2,1,0:T(8,128)(2,1)S(1)}, bf16[8,36,864]{2,1,0:T(8,128)(2,1)S(1)}, bf16[768,1440]{1,0:T(8,128)(2,1)S(1)}, bf16[416,384]{1,0:T(8...) custom-call(s32[1]{0:T(128)S(6)} %copy.13.valid_ref, ...), custom_call_target="tpu_custom_call" | custom-call | flops 4000000000 | bytes 8000000 | tf_op jit(solution)/shard_map/pallas_call | solution.py:407
  35.4 1.9 %shard_map.106 = (bf16[196,928]{1,0:T(8,128)(2,1)S(1)}, f32[208,768]{1,0:T(8,128)S(1)}) custom-call(bf16[768,1440]{1,0:T(8,128)(2,1)S(1)} %get-tuple-element.36.w_ref, bf16[416,384]{1,0:T(8,128)(2,1)S(1)} %get-tuple-element.37.dq_ref, bf16[256,608]{1,0:T(8,128)(2,1)S(1)} %get-tuple-element.38.e_ref, bf16[416,288]{1,0:T(8,128)(2,1)S(1)} %get-tuple-element.39.mixed_ref, ...), custom_call_target="tpu_custom_call" | custom-call | flops 1200000000 | bytes 4000000 | tf_op jit(solution)/shard_map/pallas_call | solution.py:407
  37.3 1.6 %collective-permute-start.17 = (bf16[196,928]{1,0:T(8,128)(2,1)S(1)}, bf16[196,928]{1,0:T(8,128)(2,1)S(1)}, u32[]{:S(2)}, u32[]{:S(2)}) collective-permute-start(bf16[196,928]{1,0:T(8,128)(2,1)S(1)} %get-tuple-element.40), channel_id=1, source_target_pairs={{0,1},{1,0},{2,3},{3,2},{4,5},{5,4},{6,7},{7,6},{8,9},{9,8},{10,11... | collective-permute-start | bytes 1091336 | tf_op jit(solution)/shard_map/ppermute | solution.py:166
  39.2 1.6 %collective-permute-start.20 = (bf16[36,864]{1,0:T(8,128)(2,1)S(1)}, bf16[36,864]{1,0:T(8,128)(2,1)S(1)}, u32[]{:S(2)}, u32[]{:S(2)}) collective-permute-start(bf16[36,864]{1,0:T(8,128)(2,1)S(1)} %get-tuple-element.52), channel_id=1, source_target_pairs={{0,4},{1,5},{2,6},{3,7},{4,0},{5,1},{6,2},{7,3},{8,12},{9,13},{10,... | collective-permute-start | bytes 186632 | tf_op jit(solution)/shard_map/ppermute | solution.py:166
  41.3 1.5 %collective-permute-start.24 = (bf16[36,864]{1,0:T(8,128)(2,1)S(1)}, bf16[36,864]{1,0:T(8,128)(2,1)S(1)}, u32[]{:S(2)}, u32[]{:S(2)}) collective-permute-start(bf16[36,864]{1,0:T(8,128)(2,1)S(1)} %get-tuple-element.56), channel_id=1, source_target_pairs={{0,4},{1,5},{2,6},{3,7},{4,0},{5,1},{6,2},{7,3},{8,12},{9,13},{10,... | collective-permute-start | bytes 186632 | tf_op jit(solution)/shard_map/ppermute | solution.py:166
  44.4 3.6 %collective-permute-start.21 = (bf16[36,864]{1,0:T(8,128)(2,1)S(1)}, bf16[36,864]{1,0:T(8,128)(2,1)S(1)}, u32[]{:S(2)}, u32[]{:S(2)}) collective-permute-start(bf16[36,864]{1,0:T(8,128)(2,1)S(1)} %shard_map.110), channel_id=1, source_target_pairs={{0,24},{1,25},{2,26},{3,27},{4,28},{5,29},{6,30},{7,31},{8,16},{9,... | collective-permute-start | bytes 186632 | tf_op jit(solution)/shard_map/ppermute | solution.py:166
  48.6 1.5 %collective-permute-start.25 = (bf16[36,864]{1,0:T(8,128)(2,1)S(1)}, bf16[36,864]{1,0:T(8,128)(2,1)S(1)}, u32[]{:S(2)}, u32[]{:S(2)}) collective-permute-start(bf16[36,864]{1,0:T(8,128)(2,1)S(1)} %shard_map.112), channel_id=1, source_target_pairs={{0,8},{1,9},{2,10},{3,11},{4,12},{5,13},{6,14},{7,15},{8,0},{9,1},... | collective-permute-start | bytes 186632 | tf_op jit(solution)/shard_map/ppermute | solution.py:166
  50.7 2.7 %collective-permute-done.23.refs_3_ = bf16[36,864]{1,0:T(8,128)(2,1)S(1)} collective-permute-done((bf16[36,864]{1,0:T(8,128)(2,1)S(1)}, bf16[36,864]{1,0:T(8,128)(2,1)S(1)}, u32[]{:S(2)}, u32[]{:S(2)}) %collective-permute-start.23) | collective-permute-done | bytes 62240 | tf_op jit(solution)/shard_map/ppermute | solution.py:166
  54.4 1.1 %shard_map.107 = (f32[196,576]{1,0:T(8,128)S(1)}, bf16[288,576]{1,0:T(8,128)(2,1)S(1)}) custom-call(bf16[768,1440]{1,0:T(8,128)(2,1)S(1)} %get-tuple-element.36.w_ref, f32[208,768]{1,0:T(8,128)S(1)} %get-tuple-element.41.dn_ref, bf16[576,768]{1,0:T(8,128)(2,1)S(1)} %get-tuple-element.35.order_ref), custom_call_target="tpu_custom_call" | custom-call | flops 600000000 | bytes 3000000 | tf_op jit(solution)/shard_map/pallas_call | solution.py:407
  55.6 1.3 %shard_map.108 = (bf16[196,576]{1,0:T(8,128)(2,1)}, bf16[196,576]{1,0:T(8,128)(2,1)}) custom-call(bf16[196,576]{1,0:T(8,128)(2,1)S(1)} %bitcast.6, bf16[196,576]{1,0:T(8,128)(2,1)S(1)} %bitcast.9, bf16[196,576]{1,0:T(8,128)(2,1)S(1)} %bitcast.10, f32[576]{0:T(1024)S(1)} %copy-done.6, bf16[196,928]{1,0:T(8,128)(2,1)S(1)} %collective-permute-done.17.got_ref, ...), custom_call_target="tpu_custom_call" | custom-call | flops 300000000 | bytes 3000000 | tf_op jit(solution)/shard_map/pallas_call | solution.py:407
  56.9 1.2 %collective-permute-done.26.cross_ref = f32[36,288]{1,0:T(8,128)S(1)} collective-permute-done((f32[36,288]{1,0:T(8,128)S(1)}, f32[36,288]{1,0:T(8,128)S(1)}, u32[]{:S(2)}, u32[]{:S(2)}) %collective-permute-start.26) | collective-permute-done | bytes 41504 | tf_op jit(solution)/shard_map/ppermute | solution.py:166
  (60 shorter events, 9.9 us)
Async XLA Ops:
  2.4 10.4 %collective-permute-start.5 = (bf16[36,1440]{1,0:T(8,128)(2,1)}, bf16[36,1440]{1,0:T(8,128)(2,1)S(1)}, u32[]{:S(2)}, u32[]{:S(2)}) collective-permute-start(bf16[36,1440]{1,0:T(8,128)(2,1)} %shard_map.104.rest_0_), channel_id=1, source_target_pairs={{0,16},{1,17},{2,18},{3,19},{4,20},{5,21},{6,22},{7,23},{8,24},{9,... | collective-permute-start | bytes 311048 | tf_op jit(solution)/shard_map/ppermute | solution.py:166
  6.6 6.3 %collective-permute-start.9 = (bf16[36,1440]{1,0:T(8,128)(2,1)}, bf16[36,1440]{1,0:T(8,128)(2,1)S(1)}, u32[]{:S(2)}, u32[]{:S(2)}) collective-permute-start(bf16[36,1440]{1,0:T(8,128)(2,1)} %shard_map.104.rest_0_), channel_id=1, source_target_pairs={{0,2},{1,3},{2,0},{3,1},{4,6},{5,7},{6,4},{7,5},{8,10},{9,11},{10,... | collective-permute-start | bytes 311048 | tf_op jit(solution)/shard_map/ppermute | solution.py:166
  6.6 7.4 %collective-permute-start.3 = (bf16[36,1440]{1,0:T(8,128)(2,1)}, bf16[36,1440]{1,0:T(8,128)(2,1)S(1)}, u32[]{:S(2)}, u32[]{:S(2)}) collective-permute-start(bf16[36,1440]{1,0:T(8,128)(2,1)} %shard_map.104.rest_0_), channel_id=1, source_target_pairs={{0,8},{1,9},{2,10},{3,11},{4,12},{5,13},{6,14},{7,15},{8,0},{9,1},... | collective-permute-start | bytes 311048 | tf_op jit(solution)/shard_map/ppermute | solution.py:166
  8.2 7.4 %collective-permute-start.2 = (bf16[36,1440]{1,0:T(8,128)(2,1)}, bf16[36,1440]{1,0:T(8,128)(2,1)S(1)}, u32[]{:S(2)}, u32[]{:S(2)}) collective-permute-start(bf16[36,1440]{1,0:T(8,128)(2,1)} %shard_map.104.rest_0_), channel_id=1, source_target_pairs={{0,4},{1,5},{2,6},{3,7},{4,0},{5,1},{6,2},{7,3},{8,12},{9,13},{10,... | collective-permute-start | bytes 311048 | tf_op jit(solution)/shard_map/ppermute | solution.py:166
  9.6 14.7 %collective-permute-start = (bf16[196,576]{1,0:T(8,128)(2,1)}, bf16[196,576]{1,0:T(8,128)(2,1)S(1)}, u32[]{:S(2)}, u32[]{:S(2)}) collective-permute-start(bf16[196,576]{1,0:T(8,128)(2,1)} %bitcast.7), channel_id=1, source_target_pairs={{0,1},{1,0},{2,3},{3,2},{4,5},{5,4},{6,7},{7,6},{8,9},{9,8},{10,11... | collective-permute-start | bytes 677384 | tf_op jit(solution)/shard_map/ppermute | solution.py:166
  12.8 5.7 %collective-permute-start.7 = (bf16[36,1440]{1,0:T(8,128)(2,1)S(1)}, bf16[36,1440]{1,0:T(8,128)(2,1)S(1)}, u32[]{:S(2)}, u32[]{:S(2)}) collective-permute-start(bf16[36,1440]{1,0:T(8,128)(2,1)S(1)} %collective-permute-done.5.rest_4_), channel_id=1, source_target_pairs={{0,8},{1,9},{2,10},{3,11},{4,12},{5,13},{6,14},{7,15},{8,0},{9,1},... | collective-permute-start | bytes 311048 | tf_op jit(solution)/shard_map/ppermute | solution.py:166
  14.0 6.1 %collective-permute-start.6 = (bf16[36,1440]{1,0:T(8,128)(2,1)S(1)}, bf16[36,1440]{1,0:T(8,128)(2,1)S(1)}, u32[]{:S(2)}, u32[]{:S(2)}) collective-permute-start(bf16[36,1440]{1,0:T(8,128)(2,1)S(1)} %collective-permute-done.5.rest_4_), channel_id=1, source_target_pairs={{0,4},{1,5},{2,6},{3,7},{4,0},{5,1},{6,2},{7,3},{8,12},{9,13},{10,... | collective-permute-start | bytes 311048 | tf_op jit(solution)/shard_map/ppermute | solution.py:166
  15.5 4.6 %collective-permute-start.11 = (bf16[36,1440]{1,0:T(8,128)(2,1)S(1)}, bf16[36,1440]{1,0:T(8,128)(2,1)S(1)}, u32[]{:S(2)}, u32[]{:S(2)}) collective-permute-start(bf16[36,1440]{1,0:T(8,128)(2,1)S(1)} %collective-permute-done.3.rest_2_), channel_id=1, source_target_pairs={{0,2},{1,3},{2,0},{3,1},{4,6},{5,7},{6,4},{7,5},{8,10},{9,11},{10,... | collective-permute-start | bytes 311048 | tf_op jit(solution)/shard_map/ppermute | solution.py:166
  15.5 14.6 %collective-permute-start.1 = (bf16[196,576]{1,0:T(8,128)(2,1)}, bf16[196,576]{1,0:T(8,128)(2,1)S(1)}, u32[]{:S(2)}, u32[]{:S(2)}) collective-permute-start(bf16[196,576]{1,0:T(8,128)(2,1)} %bitcast.11), channel_id=1, source_target_pairs={{0,1},{1,0},{2,3},{3,2},{4,5},{5,4},{6,7},{7,6},{8,9},{9,8},{10,11... | collective-permute-start | bytes 677384 | tf_op jit(solution)/shard_map/ppermute | solution.py:166
  18.6 5.2 %collective-permute-start.4 = (bf16[36,1440]{1,0:T(8,128)(2,1)S(1)}, bf16[36,1440]{1,0:T(8,128)(2,1)S(1)}, u32[]{:S(2)}, u32[]{:S(2)}) collective-permute-start(bf16[36,1440]{1,0:T(8,128)(2,1)S(1)} %collective-permute-done.3.rest_2_), channel_id=1, source_target_pairs={{0,4},{1,5},{2,6},{3,7},{4,0},{5,1},{6,2},{7,3},{8,12},{9,13},{10,... | collective-permute-start | bytes 311048 | tf_op jit(solution)/shard_map/ppermute | solution.py:166
  20.1 6.0 %collective-permute-start.8 = (bf16[36,1440]{1,0:T(8,128)(2,1)S(1)}, bf16[36,1440]{1,0:T(8,128)(2,1)S(1)}, u32[]{:S(2)}, u32[]{:S(2)}) collective-permute-start(bf16[36,1440]{1,0:T(8,128)(2,1)S(1)} %collective-permute-done.7.rest_6_), channel_id=1, source_target_pairs={{0,4},{1,5},{2,6},{3,7},{4,0},{5,1},{6,2},{7,3},{8,12},{9,13},{10,... | collective-permute-start | bytes 311048 | tf_op jit(solution)/shard_map/ppermute | solution.py:166
  23.8 6.4 %collective-permute-start.15 = (bf16[36,1440]{1,0:T(8,128)(2,1)S(1)}, bf16[36,1440]{1,0:T(8,128)(2,1)S(1)}, u32[]{:S(2)}, u32[]{:S(2)}) collective-permute-start(bf16[36,1440]{1,0:T(8,128)(2,1)S(1)} %collective-permute-done.7.rest_6_), channel_id=1, source_target_pairs={{0,2},{1,3},{2,0},{3,1},{4,6},{5,7},{6,4},{7,5},{8,10},{9,11},{10,... | collective-permute-start | bytes 311048 | tf_op jit(solution)/shard_map/ppermute | solution.py:166
  23.8 6.4 %collective-permute-start.14 = (bf16[36,1440]{1,0:T(8,128)(2,1)S(1)}, bf16[36,1440]{1,0:T(8,128)(2,1)S(1)}, u32[]{:S(2)}, u32[]{:S(2)}) collective-permute-start(bf16[36,1440]{1,0:T(8,128)(2,1)S(1)} %collective-permute-done.6.rest_5_), channel_id=1, source_target_pairs={{0,2},{1,3},{2,0},{3,1},{4,6},{5,7},{6,4},{7,5},{8,10},{9,11},{10,... | collective-permute-start | bytes 311048 | tf_op jit(solution)/shard_map/ppermute | solution.py:166
  24.3 5.9 %collective-permute-start.12 = (bf16[36,1440]{1,0:T(8,128)(2,1)S(1)}, bf16[36,1440]{1,0:T(8,128)(2,1)S(1)}, u32[]{:S(2)}, u32[]{:S(2)}) collective-permute-start(bf16[36,1440]{1,0:T(8,128)(2,1)S(1)} %collective-permute-done.4.rest_3_), channel_id=1, source_target_pairs={{0,2},{1,3},{2,0},{3,1},{4,6},{5,7},{6,4},{7,5},{8,10},{9,11},{10,... | collective-permute-start | bytes 311048 | tf_op jit(solution)/shard_map/ppermute | solution.py:166
  34.8 4.1 %collective-permute-start.18 = (bf16[8,36,864]{2,0,1:T(8,128)(2,1)S(1)}, bf16[8,36,864]{2,0,1:T(8,128)(2,1)S(1)}, u32[]{:S(2)}, u32[]{:S(2)}) collective-permute-start(bf16[8,36,864]{2,0,1:T(8,128)(2,1)S(1)} %copy.11), channel_id=1, source_target_pairs={{0,2},{1,3},{2,0},{3,1},{4,6},{5,7},{6,4},{7,5},{8,10},{9,11},{10,... | collective-permute-start | bytes 1493000 | tf_op jit(solution)/shard_map/ppermute | solution.py:166
  37.3 18.2 %collective-permute-start.17 = (bf16[196,928]{1,0:T(8,128)(2,1)S(1)}, bf16[196,928]{1,0:T(8,128)(2,1)S(1)}, u32[]{:S(2)}, u32[]{:S(2)}) collective-permute-start(bf16[196,928]{1,0:T(8,128)(2,1)S(1)} %get-tuple-element.40), channel_id=1, source_target_pairs={{0,1},{1,0},{2,3},{3,2},{4,5},{5,4},{6,7},{7,6},{8,9},{9,8},{10,11... | collective-permute-start | bytes 1091336 | tf_op jit(solution)/shard_map/ppermute | solution.py:166
  39.2 5.2 %collective-permute-start.20 = (bf16[36,864]{1,0:T(8,128)(2,1)S(1)}, bf16[36,864]{1,0:T(8,128)(2,1)S(1)}, u32[]{:S(2)}, u32[]{:S(2)}) collective-permute-start(bf16[36,864]{1,0:T(8,128)(2,1)S(1)} %get-tuple-element.52), channel_id=1, source_target_pairs={{0,4},{1,5},{2,6},{3,7},{4,0},{5,1},{6,2},{7,3},{8,12},{9,13},{10,... | collective-permute-start | bytes 186632 | tf_op jit(solution)/shard_map/ppermute | solution.py:166
  40.7 7.2 %collective-permute-start.22 = (bf16[36,864]{1,0:T(8,128)(2,1)S(1)}, bf16[36,864]{1,0:T(8,128)(2,1)S(1)}, u32[]{:S(2)}, u32[]{:S(2)}) collective-permute-start(bf16[36,864]{1,0:T(8,128)(2,1)S(1)} %get-tuple-element.54), channel_id=1, source_target_pairs={{0,4},{1,5},{2,6},{3,7},{4,0},{5,1},{6,2},{7,3},{8,12},{9,13},{10,... | collective-permute-start | bytes 186632 | tf_op jit(solution)/shard_map/ppermute | solution.py:166
  41.3 7.3 %collective-permute-start.24 = (bf16[36,864]{1,0:T(8,128)(2,1)S(1)}, bf16[36,864]{1,0:T(8,128)(2,1)S(1)}, u32[]{:S(2)}, u32[]{:S(2)}) collective-permute-start(bf16[36,864]{1,0:T(8,128)(2,1)S(1)} %get-tuple-element.56), channel_id=1, source_target_pairs={{0,4},{1,5},{2,6},{3,7},{4,0},{5,1},{6,2},{7,3},{8,12},{9,13},{10,... | collective-permute-start | bytes 186632 | tf_op jit(solution)/shard_map/ppermute | solution.py:166
  42.8 7.3 %collective-permute-start.19 = (bf16[36,864]{1,0:T(8,128)(2,1)S(1)}, bf16[36,864]{1,0:T(8,128)(2,1)S(1)}, u32[]{:S(2)}, u32[]{:S(2)}) collective-permute-start(bf16[36,864]{1,0:T(8,128)(2,1)S(1)} %get-tuple-element.50), channel_id=1, source_target_pairs={{0,4},{1,5},{2,6},{3,7},{4,0},{5,1},{6,2},{7,3},{8,12},{9,13},{10,... | collective-permute-start | bytes 186632 | tf_op jit(solution)/shard_map/ppermute | solution.py:166
  44.4 6.3 %collective-permute-start.21 = (bf16[36,864]{1,0:T(8,128)(2,1)S(1)}, bf16[36,864]{1,0:T(8,128)(2,1)S(1)}, u32[]{:S(2)}, u32[]{:S(2)}) collective-permute-start(bf16[36,864]{1,0:T(8,128)(2,1)S(1)} %shard_map.110), channel_id=1, source_target_pairs={{0,24},{1,25},{2,26},{3,27},{4,28},{5,29},{6,30},{7,31},{8,16},{9,... | collective-permute-start | bytes 186632 | tf_op jit(solution)/shard_map/ppermute | solution.py:166
  48.0 5.4 %collective-permute-start.23 = (bf16[36,864]{1,0:T(8,128)(2,1)S(1)}, bf16[36,864]{1,0:T(8,128)(2,1)S(1)}, u32[]{:S(2)}, u32[]{:S(2)}) collective-permute-start(bf16[36,864]{1,0:T(8,128)(2,1)S(1)} %shard_map.111), channel_id=1, source_target_pairs={{0,16},{1,17},{2,18},{3,19},{4,20},{5,21},{6,22},{7,23},{8,24},{9,... | collective-permute-start | bytes 186632 | tf_op jit(solution)/shard_map/ppermute | solution.py:166
  48.6 5.2 %collective-permute-start.25 = (bf16[36,864]{1,0:T(8,128)(2,1)S(1)}, bf16[36,864]{1,0:T(8,128)(2,1)S(1)}, u32[]{:S(2)}, u32[]{:S(2)}) collective-permute-start(bf16[36,864]{1,0:T(8,128)(2,1)S(1)} %shard_map.112), channel_id=1, source_target_pairs={{0,8},{1,9},{2,10},{3,11},{4,12},{5,13},{6,14},{7,15},{8,0},{9,1},... | collective-permute-start | bytes 186632 | tf_op jit(solution)/shard_map/ppermute | solution.py:166
  53.9 4.3 %collective-permute-start.26 = (f32[36,288]{1,0:T(8,128)S(1)}, f32[36,288]{1,0:T(8,128)S(1)}, u32[]{:S(2)}, u32[]{:S(2)}) collective-permute-start(f32[36,288]{1,0:T(8,128)S(1)} %get-tuple-element.58), channel_id=1, source_target_pairs={{0,1},{1,0},{2,3},{3,2},{4,5},{5,4},{6,7},{7,6},{8,9},{9,8},{10,11... | collective-permute-start | bytes 124424 | tf_op jit(solution)/shard_map/ppermute | solution.py:166
  (11 other events, 88.8 us)
where the time goes:
time: 59.1 us; the launch traced here: 58.9 us
  starting transfers between devices  27.8 us (47%)
  Pallas kernels  14.2 us (24%)
  waiting for transfers between devices  13.6 us (23%)
  local copies, waits for them, and re-layouts  1.79 us (3%)
  between operations  1.51 us (3%)
    ppermute x27, starting transfers between devices, swap(): return lax.ppermute(array, AXES, [(i, i ^ mask) for i in range(32)])  27.8 us
    pallas_call x12, Pallas kernels, call(): pl.pallas_call(kernel, out_shape=outs, in_specs=[pl.BlockSpec(memory_spac...  14.2 us
    ppermute x27, waiting for transfers between devices, swap(): return lax.ppermute(array, AXES, [(i, i ^ mask) for i in range(32)])  13.6 us
    unnamed x16, local copies, waits for them, and re-layouts  1.67 us
  transfers between devices with their start and end apart: 27, of which 10 were waited for; matrix products, arithmetic and copies ran while one was open for 0% of the time, Pallas kernels for 12%

commit v1 on v0

--- a/solution.py
+++ b/solution.py
@@ -158,7 +158,7 @@
 KLANES = HERE * KEYS
 QKV = 3 * HALF
 SHARD = QKV + D
-SEND = 640 + HALF
+SEND = D + HALF
 BF16, F32 = jnp.bfloat16, jnp.float32
 
 
@@ -170,7 +170,6 @@
     return lax.dot_general(a, b, (dims, ((), ())), preferred_element_type=F32)
 
 
-SLOTS = ("o", "x", "a", "xa", "b", "xb", "ab", "xab")
 NT = ((1,), (1,))
 TN = ((0,), (0,))
 
@@ -229,6 +228,11 @@
     centered = values - jnp.mean(values, axis=-1, keepdims=True)
     inverse = lax.rsqrt(jnp.mean(centered * centered, axis=-1, keepdims=True) + 1e-05)
     return centered * inverse, inverse
+
+
+def warm_kernel(second_ref, gain_ref, second_out, gain_out):
+    second_out[...] = second_ref[...]
+    gain_out[...] = gain_ref[...]
 
 
 def prep_kernel(own_ref, peer_ref, gain_ref, rel_ref, relt_ref, pool_ref, poolt_ref, order_ref):
@@ -328,21 +332,24 @@
         goth_ref[s] = g_ref[(s + 8) * SLOT : (s + 8) * SLOT + ROWS, :].astype(BF16)
 
 
-def cross_kernel(w_ref, dq_ref, e_ref, mixed_ref, order_ref, send_ref, dn_ref):
-    spread = one_hot(key_of_token((TOK2, 1), 0) == iota((TOK2, KEYS), 1))
-    d_tokens = dot(spread, e_ref[:KEYS, :]).astype(BF16)
-    d_normed = dot(dq_ref[...], w_ref[:, :384], NT) + dot(d_tokens, w_ref[:, 256:QKV], NT)
-    dn_ref[...] = d_normed[:FSLOT]
-    peer = dot(d_normed[FSLOT:].astype(BF16), order_ref[...], NT)
+def d_normed_of(f, w_ref, dq_ref, e_ref):
+    rows = slice(f * FSLOT, (f + 1) * FSLOT)
+    keys = key_of_token((TOK2, 1), 0)[rows]
+    d_tokens = dot(one_hot(keys == iota((FSLOT, KEYS), 1)), e_ref[:KEYS, :]).astype(BF16)
+    return dot(dq_ref[rows, :], w_ref[:, :384], NT) + dot(d_tokens, w_ref[:, 256:QKV], NT)
+
+
+def cross_kernel(w_ref, dq_ref, e_ref, mixed_ref, order_ref, send_ref):
+    peer = dot(d_normed_of(1, w_ref, dq_ref, e_ref).astype(BF16), order_ref[...], NT)
     send_ref[:, :D] = peer[:FRAME_TOK].astype(BF16)
-    send_ref[:, D:640] = jnp.zeros((FRAME_TOK, 640 - D), BF16)
-    send_ref[:, 640:] = mixed_ref[FSLOT : FSLOT + FRAME_TOK, :]
-
-
-def late_kernel(w_ref, dn_ref, order_ref, nat_ref, oth_ref):
+    send_ref[:, D:] = mixed_ref[FSLOT : FSLOT + FRAME_TOK, :]
+
+
+def late_kernel(w_ref, dq_ref, e_ref, order_ref, nat_ref, oth_ref):
     order = order_ref[...]
-    hi = dn_ref[...].astype(BF16)
-    lo = (dn_ref[...] - hi.astype(F32)).astype(BF16)
+    own = d_normed_of(0, w_ref, dq_ref, e_ref)
+    hi = own.astype(BF16)
+    lo = (own - hi.astype(F32)).astype(BF16)
     nat_ref[...] = (dot(hi, order, NT) + dot(lo, order, NT))[:FRAME_TOK]
     other = 1 - lax.axis_index("seq")
     select = order_ref[pl.ds(pl.multiple_of(other * HALF, HALF), HALF), :]
@@ -350,7 +357,7 @@
 
 
 def last_kernel(yone_ref, second_ref, dtwo_ref, gain_ref, got_ref, dn_ref, mixed_ref, outh_ref, oth_ref, x_ref, dx_ref):
-    branch = dot(mixed_ref[:FRAME_TOK, :], outh_ref[...]) + dot(got_ref[:, 640:], oth_ref[...])
+    branch = dot(mixed_ref[:FRAME_TOK, :], outh_ref[...]) + dot(got_ref[:, D:], oth_ref[...])
     x_ref[...] = (yone_ref[...].astype(F32) - branch).astype(BF16)
     xhat, inverse = standardize(second_ref[...].astype(F32))
     gained = (dn_ref[...] + got_ref[:, :D].astype(F32)) * gain_ref[...].reshape(1, D)
@@ -362,46 +369,61 @@
     dx_ref[...] = (dtwo_ref[...].astype(F32) + lower).astype(BF16)
 
 
-def split_kernel(own_ref, got_ref, *outs):
-    for s in range(8):
-        outs[s][...] = (own_ref[s].astype(F32) + got_ref[s].astype(F32)).astype(BF16)
-
-
-def add_kernel(a_ref, b_ref, sum_ref):
-    sum_ref[...] = (a_ref[...].astype(F32) + b_ref[...].astype(F32)).astype(BF16)
-
-
-def sum_kernel(*refs):
-    terms, (total_ref, cross_ref) = refs[:-2], refs[-2:]
-    total = sum(t[...].astype(F32) for t in terms)
-    total_ref[...] = total
+def split_kernel(own_ref, got_ref, kept_ref, xab_ref, xb_ref, near_ref):
+    for ref, s in (
+        (xab_ref, 7),
+        (xb_ref, 5),
+        (near_ref.at[0], 3),
+        (near_ref.at[1], 1),
+        (kept_ref.at[3], 6),
+        (kept_ref.at[2], 4),
+        (kept_ref.at[1], 2),
+        (kept_ref.at[0], 0),
+    ):
+        ref[...] = (own_ref[s].astype(F32) + got_ref[s].astype(F32)).astype(BF16)
+
+
+def store_parts(total, cross_ref, stay_ref):
     y = lax.axis_index("seq")
 
     @pl.when(y == 0)
     def _():
-        cross_ref[...] = total[:, 2 * HALF :]
+        cross_ref[...] = total[:, 2 * HALF :].astype(cross_ref.dtype)
+        stay_ref[...] = total[:, : 2 * HALF].astype(stay_ref.dtype)
 
     @pl.when(y == 1)
     def _():
-        cross_ref[...] = total[:, :HALF]
-
-
-def join_kernel(total_ref, cross_ref, grad_ref):
-    y = lax.axis_index("seq")
-    grad_ref[:, HALF : 2 * HALF] = cross_ref[...]
-    for s in range(2):
-
-        @pl.when(y == s)
-        def _():
-            grad_ref[:, :HALF] = total_ref[:, s * HALF : (s + 1) * HALF]
-            grad_ref[:, 2 * HALF :] = total_ref[:, (s + 1) * HALF : (s + 2) * HALF]
+        cross_ref[...] = total[:, :HALF].astype(cross_ref.dtype)
+        stay_ref[...] = total[:, HALF:].astype(stay_ref.dtype)
+
+
+def add_kernel(at, kept_ref, got_ref, sum_ref):
+    sum_ref[...] = (kept_ref[at].astype(F32) + got_ref[...].astype(F32)).astype(BF16)
+
+
+def near_kernel(kept_ref, got_ref, a_ref, o_ref):
+    a_ref[...] = (kept_ref[1].astype(F32) + got_ref[0].astype(F32)).astype(BF16)
+    o_ref[...] = kept_ref[0].astype(F32) + got_ref[1].astype(F32)
+
+
+def sum_kernel(o_ref, a_ref, ab_ref, b_ref, cross_ref, stay_ref):
+    total = o_ref[...] + a_ref[...].astype(F32) + ab_ref[...].astype(F32) + b_ref[...].astype(F32)
+    store_parts(total, cross_ref, stay_ref)
+
+
+def join_kernel(crossed_ref, *refs):
+    grad_ref = refs[-1]
+    total = sum(term[...].astype(F32) for term in refs[:-1])
+    grad_ref[:, :HALF] = total[:, :HALF]
+    grad_ref[:, HALF : 2 * HALF] = crossed_ref[...].astype(F32)
+    grad_ref[:, 2 * HALF :] = total[:, HALF:]
 
 
 def shape(*dims, kind=BF16):
     return jax.ShapeDtypeStruct(dims, kind)
 
 
-def call(kernel, outs, args, scratch=(), smem=0, hbm=False, flops=0, moved=0, limit=16):
+def call(kernel, outs, args, scratch=(), smem=0, hbm=False, flops=0, moved=0, limit=16 << 10):
     vmem = pl.BlockSpec(memory_space=pltpu.VMEM)
     source = pl.BlockSpec(memory_space=pltpu.HBM) if hbm else vmem
     return pl.pallas_call(
@@ -410,7 +432,7 @@
         in_specs=[pl.BlockSpec(memory_space=pltpu.SMEM)] * smem + [source] * (len(args) - smem),
         out_specs=jax.tree.map(lambda _: vmem, outs),
         scratch_shapes=scratch,
-        compiler_params=pltpu.CompilerParams(vmem_limit_bytes=limit << 20),
+        compiler_params=pltpu.CompilerParams(vmem_limit_bytes=limit << 10),
         cost_estimate=pl.CostEstimate(flops=flops, bytes_accessed=moved, transcendentals=0),
     )(*args)
 
@@ -431,7 +453,7 @@
         ),
         hbm=True,
         moved=400_000,
-        limit=60,
+        limit=60 << 10,
     )
     by_b = swap(own, OVER_Z2)
     by_x = swap(own, OVER_X)
@@ -445,10 +467,13 @@
     mine = (own, by_x, by_a, by_xa, by_b, by_xb, by_ab, by_xab)
     other = tuple(swap(block, OVER_CORE) for block in mine)
 
+    second_here, gain_here = call(
+        warm_kernel, (shape(FRAME_TOK, D), shape(D, kind=F32)), (second, gain), moved=500_000
+    )
     rel, rel_t, pool, pool_t, order = call(
         prep_kernel,
         (shape(TOK2, REL), shape(2, REL, FSLOT), shape(2 * KEYS, REL), shape(REL, 2 * KEYS), shape(D, REL)),
-        (second, second_peer, gain),
+        (second_here, second_peer, gain_here),
         flops=1_200_000_000,
         moved=3_000_000,
     )
@@ -476,48 +501,52 @@
         smem=1,
         flops=4_000_000_000,
         moved=8_000_000,
-        limit=32,
-    )
-
-    block = shape(ROWS, QKV)
-
-    def add(a, b):
-        return call(add_kernel, block, (a, b), moved=200_000)
-
-    chunk = call(split_kernel, (block,) * 8, (g_own, swap(g_oth, OVER_CORE)), moved=1_500_000)
-    by_slot = dict(zip(SLOTS, chunk))
-    terms = [by_slot["o"], swap(by_slot["x"], OVER_X)]
-    for name, mask in (("ab", OVER_Z1 | OVER_Z2), ("b", OVER_Z2), ("a", OVER_Z1)):
-        summed = add(by_slot[name], swap(by_slot["x" + name], OVER_X))
-        terms.append(swap(summed, mask))
-    total, crossing = call(
+        limit=32 << 10,
+    )
+
+    block, pair = shape(ROWS, QKV), shape(2, ROWS, QKV)
+    wide = shape(ROWS, QKV, kind=F32)
+    kept, x_ab, x_b, near = call(
+        split_kernel,
+        (shape(4, ROWS, QKV), block, block, pair),
+        (g_own, swap(g_oth, OVER_CORE)),
+        moved=1_500_000,
+    )
+    got_ab, got_b = swap(x_ab, OVER_X), swap(x_b, OVER_X)
+    to_ab = call(functools.partial(add_kernel, 3), block, (kept, got_ab), moved=200_000)
+    to_b = call(functools.partial(add_kernel, 2), block, (kept, got_b), moved=200_000)
+    to_a, here = call(near_kernel, (block, wide), (kept, swap(near, OVER_X)), moved=400_000)
+    from_ab = swap(to_ab, OVER_Z1 | OVER_Z2)
+    from_b = swap(to_b, OVER_Z2)
+    from_a = swap(to_a, OVER_Z1)
+    crossing, stay = call(
         sum_kernel,
-        (shape(ROWS, QKV, kind=F32), shape(ROWS, HALF, kind=F32)),
-        tuple(terms),
-        moved=500_000,
+        (shape(ROWS, HALF), shape(ROWS, 2 * HALF, kind=F32)),
+        (here, from_a, from_ab, from_b),
+        moved=400_000,
     )
     crossed = swap(crossing, OVER_Y)
-    grad_qkv = call(join_kernel, shape(ROWS, QKV, kind=F32), (total, crossed), moved=300_000)
-
-    send, d_normed = call(
+    grad_qkv = call(join_kernel, wide, (crossed, stay), moved=300_000)
+
+    send = call(
         cross_kernel,
-        (shape(FRAME_TOK, SEND), shape(FSLOT, REL, kind=F32)),
+        shape(FRAME_TOK, SEND),
         (w_rel, d_q, e, mixed, order),
-        flops=1_200_000_000,
+        flops=600_000_000,
         moved=4_000_000,
     )
     got = swap(send, OVER_Y)
     d_normed, out_oth = call(
         late_kernel,
         (shape(FRAME_TOK, D, kind=F32), shape(HALF, D)),
-        (w_rel, d_normed, order),
-        flops=600_000_000,
+        (w_rel, d_q, e, order),
+        flops=1_000_000_000,
         moved=3_000_000,
     )
     x_one, dx_two = call(
         last_kernel,
         (shape(FRAME_TOK, D), shape(FRAME_TOK, D)),
-        (y_one[0], second, d_two[0], gain, got, d_normed, mixed, out_own, out_oth),
+        (y_one[0], second_here, d_two[0], gain_here, got, d_normed, mixed, out_own, out_oth),
         flops=300_000_000,
         moved=3_000_000,
     )

time: 59.1 us -> 58.7 us (level)
  starting transfers between devices: 27.8 us -> 26.9 us
    ppermute x27 -> x26, starting transfers between devices: 27.8 us -> 26.9 us  [swap(): return lax.ppermute(array, AXES, [(i, i ^ mask) for i in range(32)])]
    pallas_call x12 -> x13, Pallas kernels: 14.2 us -> 14.6 us  [call(): pl.pallas_call(kernel, out_shape=outs, in_specs=[pl.BlockSpec(memory_spac...]
    ppermute x27 -> x26, waiting for transfers between devices: 13.6 us -> 13.7 us  [swap(): return lax.ppermute(array, AXES, [(i, i ^ mask) for i in range(32)])]
    unnamed x16 -> x12, local copies, waits for them, and re-layouts: 1.67 us -> 1.65 us
  transfers between devices with their start and end apart: 27 -> 26, of which waited for: 10 -> 8; matrix products, arithmetic and copies ran while one was open for 0% -> 0% of each run, Pallas kernels for 12% -> 13%
where the time goes in v1:
time: 58.7 us; the launch traced here: 58.5 us
  starting transfers between devices  26.9 us (46%)
  Pallas kernels  14.6 us (25%)
  waiting for transfers between devices  13.7 us (23%)
  local copies, waits for them, and re-layouts  1.77 us (3%)
  between operations  1.49 us (3%)
    ppermute x26, starting transfers between devices, swap(): return lax.ppermute(array, AXES, [(i, i ^ mask) for i in range(32)])  26.9 us
    pallas_call x13, Pallas kernels, call(): pl.pallas_call(kernel, out_shape=outs, in_specs=[pl.BlockSpec(memory_spac...  14.6 us
    ppermute x26, waiting for transfers between devices, swap(): return lax.ppermute(array, AXES, [(i, i ^ mask) for i in range(32)])  13.7 us
    unnamed x12, local copies, waits for them, and re-layouts  1.65 us
  transfers between devices with their start and end apart: 26, of which 8 were waited for; matrix products, arithmetic and copies ran while one was open for 0% of the time, Pallas kernels for 13%

profile of v1, /device:TPU:0, one launch (start us, length us, event | category | flops | bytes accessed | tf_op | source)
XLA Modules:
  0.0 58.5 jit_solution(1854355918802018058)
XLA Ops:
  0.6 1.8 %shard_map.105.rest_0_ = bf16[36,1440]{1,0:T(8,128)(2,1)} custom-call(bf16[36,1728]{1,0:T(8,128)(2,1)} %qkv_hbm.1, bf16[36,576]{1,0:T(8,128)(2,1)} %out_hbm.1), custom_call_target="tpu_custom_call" | custom-call | bytes 400000 | tf_op jit(solution)/shard_map/pallas_call | solution.py:429
  2.4 4.1 %collective-permute-start.5 = (bf16[36,1440]{1,0:T(8,128)(2,1)}, bf16[36,1440]{1,0:T(8,128)(2,1)S(1)}, u32[]{:S(2)}, u32[]{:S(2)}) collective-permute-start(bf16[36,1440]{1,0:T(8,128)(2,1)} %shard_map.105.rest_0_), channel_id=1, source_target_pairs={{0,16},{1,17},{2,18},{3,19},{4,20},{5,21},{6,22},{7,23},{8,24},{9,... | collective-permute-start | bytes 311048 | tf_op jit(solution)/shard_map/ppermute | solution.py:166
  6.6 1.6 %collective-permute-start.3 = (bf16[36,1440]{1,0:T(8,128)(2,1)}, bf16[36,1440]{1,0:T(8,128)(2,1)S(1)}, u32[]{:S(2)}, u32[]{:S(2)}) collective-permute-start(bf16[36,1440]{1,0:T(8,128)(2,1)} %shard_map.105.rest_0_), channel_id=1, source_target_pairs={{0,8},{1,9},{2,10},{3,11},{4,12},{5,13},{6,14},{7,15},{8,0},{9,1},... | collective-permute-start | bytes 311048 | tf_op jit(solution)/shard_map/ppermute | solution.py:166
  8.2 1.5 %collective-permute-start.2 = (bf16[36,1440]{1,0:T(8,128)(2,1)}, bf16[36,1440]{1,0:T(8,128)(2,1)S(1)}, u32[]{:S(2)}, u32[]{:S(2)}) collective-permute-start(bf16[36,1440]{1,0:T(8,128)(2,1)} %shard_map.105.rest_0_), channel_id=1, source_target_pairs={{0,4},{1,5},{2,6},{3,7},{4,0},{5,1},{6,2},{7,3},{8,12},{9,13},{10,... | collective-permute-start | bytes 311048 | tf_op jit(solution)/shard_map/ppermute | solution.py:166
  9.6 1.5 %collective-permute-start = (bf16[196,576]{1,0:T(8,128)(2,1)}, bf16[196,576]{1,0:T(8,128)(2,1)S(1)}, u32[]{:S(2)}, u32[]{:S(2)}) collective-permute-start(bf16[196,576]{1,0:T(8,128)(2,1)} %bitcast.8), channel_id=1, source_target_pairs={{0,1},{1,0},{2,3},{3,2},{4,5},{5,4},{6,7},{7,6},{8,9},{9,8},{10,11... | collective-permute-start | bytes 677384 | tf_op jit(solution)/shard_map/ppermute | solution.py:166
  11.2 1.7 %collective-permute-done.5.rest_4_ = bf16[36,1440]{1,0:T(8,128)(2,1)S(1)} collective-permute-done((bf16[36,1440]{1,0:T(8,128)(2,1)}, bf16[36,1440]{1,0:T(8,128)(2,1)S(1)}, u32[]{:S(2)}, u32[]{:S(2)}) %collective-permute-start.5) | collective-permute-done | bytes 103712 | tf_op jit(solution)/shard_map/ppermute | solution.py:166
  14.0 1.5 %collective-permute-start.6 = (bf16[36,1440]{1,0:T(8,128)(2,1)S(1)}, bf16[36,1440]{1,0:T(8,128)(2,1)S(1)}, u32[]{:S(2)}, u32[]{:S(2)}) collective-permute-start(bf16[36,1440]{1,0:T(8,128)(2,1)S(1)} %collective-permute-done.5.rest_4_), channel_id=1, source_target_pairs={{0,4},{1,5},{2,6},{3,7},{4,0},{5,1},{6,2},{7,3},{8,12},{9,13},{10,... | collective-permute-start | bytes 311048 | tf_op jit(solution)/shard_map/ppermute | solution.py:166
  15.5 1.6 %collective-permute-start.1 = (bf16[196,576]{1,0:T(8,128)(2,1)}, bf16[196,576]{1,0:T(8,128)(2,1)S(1)}, u32[]{:S(2)}, u32[]{:S(2)}) collective-permute-start(bf16[196,576]{1,0:T(8,128)(2,1)} %bitcast.10), channel_id=1, source_target_pairs={{0,1},{1,0},{2,3},{3,2},{4,5},{5,4},{6,7},{7,6},{8,9},{9,8},{10,11... | collective-permute-start | bytes 677384 | tf_op jit(solution)/shard_map/ppermute | solution.py:166
  17.1 1.4 %collective-permute-done.7.rest_6_ = bf16[36,1440]{1,0:T(8,128)(2,1)S(1)} collective-permute-done((bf16[36,1440]{1,0:T(8,128)(2,1)S(1)}, bf16[36,1440]{1,0:T(8,128)(2,1)S(1)}, u32[]{:S(2)}, u32[]{:S(2)}) %collective-permute-start.7) | collective-permute-done | bytes 103712 | tf_op jit(solution)/shard_map/ppermute | solution.py:166
  18.6 1.5 %collective-permute-start.4 = (bf16[36,1440]{1,0:T(8,128)(2,1)S(1)}, bf16[36,1440]{1,0:T(8,128)(2,1)S(1)}, u32[]{:S(2)}, u32[]{:S(2)}) collective-permute-start(bf16[36,1440]{1,0:T(8,128)(2,1)S(1)} %collective-permute-done.3.rest_2_), channel_id=1, source_target_pairs={{0,4},{1,5},{2,6},{3,7},{4,0},{5,1},{6,2},{7,3},{8,12},{9,13},{10,... | collective-permute-start | bytes 311048 | tf_op jit(solution)/shard_map/ppermute | solution.py:166
  24.4 1.7 %collective-permute-done.8.rest_7_ = bf16[36,1440]{1,0:T(8,128)(2,1)S(1)} collective-permute-done((bf16[36,1440]{1,0:T(8,128)(2,1)S(1)}, bf16[36,1440]{1,0:T(8,128)(2,1)S(1)}, u32[]{:S(2)}, u32[]{:S(2)}) %collective-permute-start.8) | collective-permute-done | bytes 103712 | tf_op jit(solution)/shard_map/ppermute | solution.py:166
  26.1 2.4 %shard_map.104 = (bf16[416,768]{1,0:T(8,128)(2,1)S(1)}, bf16[2,768,208]{2,1,0:T(8,128)(2,1)S(1)}, bf16[256,768]{1,0:T(8,128)(2,1)S(1)}, bf16[768,256]{1,0:T(8,128)(2,1)S(1)}, bf16[576,768]{1,0:T(8,128)(2,1)S(1)}) custom-call(bf16[196,576]{1,0:T(8,128)(2,1)S(1)} %get-tuple-element.29.own_ref.second_ref, bf16[196,576]{1,0:T(8,128)(2,1)S(1)} %collective-permute-done.peer_ref, ...), custom_call_target="tpu_custom_call" | custom-call | flops 1200000000 | bytes 3000000 | tf_op jit(solution)/shard_map/pallas_call | solution.py:429
  28.6 4.6 %shard_map.106 = (bf16[8,36,864]{2,1,0:T(8,128)(2,1)S(1)}, bf16[8,36,864]{2,1,0:T(8,128)(2,1)S(1)}, bf16[768,1440]{1,0:T(8,128)(2,1)S(1)}, bf16[416,384]{1,0:T(8...) custom-call(s32[1]{0:T(128)S(6)} %copy.13.valid_ref, ...), custom_call_target="tpu_custom_call" | custom-call | flops 4000000000 | bytes 8000000 | tf_op jit(solution)/shard_map/pallas_call | solution.py:429
  33.8 1.3 %shard_map.107 = bf16[196,864]{1,0:T(8,128)(2,1)S(1)} custom-call(bf16[768,1440]{1,0:T(8,128)(2,1)S(1)} %get-tuple-element.36.w_ref, bf16[416,384]{1,0:T(8,128)(2,1)S(1)} %get-tuple-element.37.dq_ref, bf16[256,608]{1,0:T(8,128)(2,1)S(1)} %get-tuple-element.38.e_ref, bf16[416,288]{1,0:T(8,128)(2,1)S(1)} %get-tuple-element.39.mixed_ref, ...), custom_call_target="tpu_custom_call" | custom-call | flops 600000000 | bytes 4000000 | tf_op jit(solution)/shard_map/pallas_call | solution.py:429
  35.1 1.7 %collective-permute-start.17 = (bf16[196,864]{1,0:T(8,128)(2,1)S(1)}, bf16[196,864]{1,0:T(8,128)(2,1)S(1)}, u32[]{:S(2)}, u32[]{:S(2)}) collective-permute-start(bf16[196,864]{1,0:T(8,128)(2,1)S(1)} %shard_map.107), channel_id=1, source_target_pairs={{0,1},{1,0},{2,3},{3,2},{4,5},{5,4},{6,7},{7,6},{8,9},{9,8},{10,11... | collective-permute-start | bytes 1016072 | tf_op jit(solution)/shard_map/ppermute | solution.py:166
  37.0 1.6 %collective-permute-start.19 = (bf16[2,36,864]{2,1,0:T(8,128)(2,1)S(1)}, bf16[2,36,864]{2,1,0:T(8,128)(2,1)S(1)}, u32[]{:S(2)}, u32[]{:S(2)}) collective-permute-start(bf16[2,36,864]{2,1,0:T(8,128)(2,1)S(1)} %get-tuple-element.48), channel_id=1, source_target_pairs={{0,4},{1,5},{2,6},{3,7},{4,0},{5,1},{6,2},{7,3},{8,12},{9,13},{10,... | collective-permute-start | bytes 373256 | tf_op jit(solution)/shard_map/ppermute | solution.py:166
  39.1 1.5 %collective-permute-start.23 = (bf16[36,864]{1,0:T(8,128)(2,1)S(1)}, bf16[36,864]{1,0:T(8,128)(2,1)S(1)}, u32[]{:S(2)}, u32[]{:S(2)}) collective-permute-start(bf16[36,864]{1,0:T(8,128)(2,1)S(1)} %get-tuple-element.52), channel_id=1, source_target_pairs={{0,4},{1,5},{2,6},{3,7},{4,0},{5,1},{6,2},{7,3},{8,12},{9,13},{10,... | collective-permute-start | bytes 186632 | tf_op jit(solution)/shard_map/ppermute | solution.py:166
  40.6 4.2 %collective-permute-done.21.got_ref = bf16[36,864]{1,0:T(8,128)(2,1)S(1)} collective-permute-done((bf16[36,864]{1,0:T(8,128)(2,1)S(1)}, bf16[36,864]{1,0:T(8,128)(2,1)S(1)}, u32[]{:S(2)}, u32[]{:S(2)}) %collective-permute-start.21) | collective-permute-done | bytes 62240 | tf_op jit(solution)/shard_map/ppermute | solution.py:166
  44.8 3.6 %collective-permute-start.22 = (bf16[36,864]{1,0:T(8,128)(2,1)S(1)}, bf16[36,864]{1,0:T(8,128)(2,1)S(1)}, u32[]{:S(2)}, u32[]{:S(2)}) collective-permute-start(bf16[36,864]{1,0:T(8,128)(2,1)S(1)} %shard_map.112), channel_id=1, source_target_pairs={{0,24},{1,25},{2,26},{3,27},{4,28},{5,29},{6,30},{7,31},{8,16},{9,... | collective-permute-start | bytes 186632 | tf_op jit(solution)/shard_map/ppermute | solution.py:166
  48.5 1.3 %collective-permute-start.20 = (bf16[36,864]{1,0:T(8,128)(2,1)S(1)}, bf16[36,864]{1,0:T(8,128)(2,1)S(1)}, u32[]{:S(2)}, u32[]{:S(2)}) collective-permute-start(bf16[36,864]{1,0:T(8,128)(2,1)S(1)} %get-tuple-element.50), channel_id=1, source_target_pairs={{0,8},{1,9},{2,10},{3,11},{4,12},{5,13},{6,14},{7,15},{8,0},{9,1},... | collective-permute-start | bytes 186632 | tf_op jit(solution)/shard_map/ppermute | solution.py:166
  49.8 1.9 %shard_map.108 = (f32[196,576]{1,0:T(8,128)S(1)}, bf16[288,576]{1,0:T(8,128)(2,1)S(1)}) custom-call(bf16[768,1440]{1,0:T(8,128)(2,1)S(1)} %get-tuple-element.36.w_ref, bf16[416,384]{1,0:T(8,128)(2,1)S(1)} %get-tuple-element.37.dq_ref, bf16[256,608]{1,0:T(8,128)(2,1)S(1)} %get-tuple-element.38.e_ref, bf16[576,768]{1,0:T(8,128)(2,1)S(1)} %get-tuple-element.35.order_ref), custom_call_target="tpu_custom_call" | custom-call | flops 1000000000 | bytes 3000000 | tf_op jit(solution)/shard_map/pallas_call | solution.py:429
  51.7 1.9 %collective-permute-done.24.b_ref = bf16[36,864]{1,0:T(8,128)(2,1)S(1)} collective-permute-done((bf16[36,864]{1,0:T(8,128)(2,1)S(1)}, bf16[36,864]{1,0:T(8,128)(2,1)S(1)}, u32[]{:S(2)}, u32[]{:S(2)}) %collective-permute-start.24) | collective-permute-done | bytes 62240 | tf_op jit(solution)/shard_map/ppermute | solution.py:166
  54.7 1.4 %shard_map.109 = (bf16[196,576]{1,0:T(8,128)(2,1)}, bf16[196,576]{1,0:T(8,128)(2,1)}) custom-call(bf16[196,576]{1,0:T(8,128)(2,1)S(1)} %bitcast.6, bf16[196,576]{1,0:T(8,128)(2,1)S(1)} %get-tuple-element.29.own_ref.second_ref, bf16[196,576]{1,0:T(8,128)(2,1)S(1)} %bitcast.7, f32[576]{0:T(1024)S(1)} %get-tuple-element.30.gain_ref, ...), custom_call_target="tpu_custom_call" | custom-call | flops 300000000 | bytes 3000000 | tf_op jit(solution)/shard_map/pallas_call | solution.py:429
  56.2 1.6 %collective-permute-done.25.crossed_ref = bf16[36,288]{1,0:T(8,128)(2,1)S(1)} collective-permute-done((bf16[36,288]{1,0:T(8,128)(2,1)S(1)}, bf16[36,288]{1,0:T(8,128)(2,1)S(1)}, u32[]{:S(2)}, u32[]{:S(2)}) %collective-permute-start.25) | collective-permute-done | bytes 20768 | tf_op jit(solution)/shard_map/ppermute | solution.py:166
  (55 shorter events, 8.1 us)
Async XLA Ops:
  2.4 10.4 %collective-permute-start.5 = (bf16[36,1440]{1,0:T(8,128)(2,1)}, bf16[36,1440]{1,0:T(8,128)(2,1)S(1)}, u32[]{:S(2)}, u32[]{:S(2)}) collective-permute-start(bf16[36,1440]{1,0:T(8,128)(2,1)} %shard_map.105.rest_0_), channel_id=1, source_target_pairs={{0,16},{1,17},{2,18},{3,19},{4,20},{5,21},{6,22},{7,23},{8,24},{9,... | collective-permute-start | bytes 311048 | tf_op jit(solution)/shard_map/ppermute | solution.py:166
  6.6 6.3 %collective-permute-start.9 = (bf16[36,1440]{1,0:T(8,128)(2,1)}, bf16[36,1440]{1,0:T(8,128)(2,1)S(1)}, u32[]{:S(2)}, u32[]{:S(2)}) collective-permute-start(bf16[36,1440]{1,0:T(8,128)(2,1)} %shard_map.105.rest_0_), channel_id=1, source_target_pairs={{0,2},{1,3},{2,0},{3,1},{4,6},{5,7},{6,4},{7,5},{8,10},{9,11},{10,... | collective-permute-start | bytes 311048 | tf_op jit(solution)/shard_map/ppermute | solution.py:166
  6.6 7.4 %collective-permute-start.3 = (bf16[36,1440]{1,0:T(8,128)(2,1)}, bf16[36,1440]{1,0:T(8,128)(2,1)S(1)}, u32[]{:S(2)}, u32[]{:S(2)}) collective-permute-start(bf16[36,1440]{1,0:T(8,128)(2,1)} %shard_map.105.rest_0_), channel_id=1, source_target_pairs={{0,8},{1,9},{2,10},{3,11},{4,12},{5,13},{6,14},{7,15},{8,0},{9,1},... | collective-permute-start | bytes 311048 | tf_op jit(solution)/shard_map/ppermute | solution.py:166
  8.2 7.4 %collective-permute-start.2 = (bf16[36,1440]{1,0:T(8,128)(2,1)}, bf16[36,1440]{1,0:T(8,128)(2,1)S(1)}, u32[]{:S(2)}, u32[]{:S(2)}) collective-permute-start(bf16[36,1440]{1,0:T(8,128)(2,1)} %shard_map.105.rest_0_), channel_id=1, source_target_pairs={{0,4},{1,5},{2,6},{3,7},{4,0},{5,1},{6,2},{7,3},{8,12},{9,13},{10,... | collective-permute-start | bytes 311048 | tf_op jit(solution)/shard_map/ppermute | solution.py:166
  9.6 14.7 %collective-permute-start = (bf16[196,576]{1,0:T(8,128)(2,1)}, bf16[196,576]{1,0:T(8,128)(2,1)S(1)}, u32[]{:S(2)}, u32[]{:S(2)}) collective-permute-start(bf16[196,576]{1,0:T(8,128)(2,1)} %bitcast.8), channel_id=1, source_target_pairs={{0,1},{1,0},{2,3},{3,2},{4,5},{5,4},{6,7},{7,6},{8,9},{9,8},{10,11... | collective-permute-start | bytes 677384 | tf_op jit(solution)/shard_map/ppermute | solution.py:166
  12.8 5.7 %collective-permute-start.7 = (bf16[36,1440]{1,0:T(8,128)(2,1)S(1)}, bf16[36,1440]{1,0:T(8,128)(2,1)S(1)}, u32[]{:S(2)}, u32[]{:S(2)}) collective-permute-start(bf16[36,1440]{1,0:T(8,128)(2,1)S(1)} %collective-permute-done.5.rest_4_), channel_id=1, source_target_pairs={{0,8},{1,9},{2,10},{3,11},{4,12},{5,13},{6,14},{7,15},{8,0},{9,1},... | collective-permute-start | bytes 311048 | tf_op jit(solution)/shard_map/ppermute | solution.py:166
  14.0 6.1 %collective-permute-start.6 = (bf16[36,1440]{1,0:T(8,128)(2,1)S(1)}, bf16[36,1440]{1,0:T(8,128)(2,1)S(1)}, u32[]{:S(2)}, u32[]{:S(2)}) collective-permute-start(bf16[36,1440]{1,0:T(8,128)(2,1)S(1)} %collective-permute-done.5.rest_4_), channel_id=1, source_target_pairs={{0,4},{1,5},{2,6},{3,7},{4,0},{5,1},{6,2},{7,3},{8,12},{9,13},{10,... | collective-permute-start | bytes 311048 | tf_op jit(solution)/shard_map/ppermute | solution.py:166
  15.5 4.6 %collective-permute-start.11 = (bf16[36,1440]{1,0:T(8,128)(2,1)S(1)}, bf16[36,1440]{1,0:T(8,128)(2,1)S(1)}, u32[]{:S(2)}, u32[]{:S(2)}) collective-permute-start(bf16[36,1440]{1,0:T(8,128)(2,1)S(1)} %collective-permute-done.3.rest_2_), channel_id=1, source_target_pairs={{0,2},{1,3},{2,0},{3,1},{4,6},{5,7},{6,4},{7,5},{8,10},{9,11},{10,... | collective-permute-start | bytes 311048 | tf_op jit(solution)/shard_map/ppermute | solution.py:166
  15.5 13.0 %collective-permute-start.1 = (bf16[196,576]{1,0:T(8,128)(2,1)}, bf16[196,576]{1,0:T(8,128)(2,1)S(1)}, u32[]{:S(2)}, u32[]{:S(2)}) collective-permute-start(bf16[196,576]{1,0:T(8,128)(2,1)} %bitcast.10), channel_id=1, source_target_pairs={{0,1},{1,0},{2,3},{3,2},{4,5},{5,4},{6,7},{7,6},{8,9},{9,8},{10,11... | collective-permute-start | bytes 677384 | tf_op jit(solution)/shard_map/ppermute | solution.py:166
  18.6 5.2 %collective-permute-start.4 = (bf16[36,1440]{1,0:T(8,128)(2,1)S(1)}, bf16[36,1440]{1,0:T(8,128)(2,1)S(1)}, u32[]{:S(2)}, u32[]{:S(2)}) collective-permute-start(bf16[36,1440]{1,0:T(8,128)(2,1)S(1)} %collective-permute-done.3.rest_2_), channel_id=1, source_target_pairs={{0,4},{1,5},{2,6},{3,7},{4,0},{5,1},{6,2},{7,3},{8,12},{9,13},{10,... | collective-permute-start | bytes 311048 | tf_op jit(solution)/shard_map/ppermute | solution.py:166
  20.1 3.7 %collective-permute-start.10 = (bf16[36,1440]{1,0:T(8,128)(2,1)S(1)}, bf16[36,1440]{1,0:T(8,128)(2,1)S(1)}, u32[]{:S(2)}, u32[]{:S(2)}) collective-permute-start(bf16[36,1440]{1,0:T(8,128)(2,1)S(1)} %collective-permute-done.2.rest_1_), channel_id=1, source_target_pairs={{0,2},{1,3},{2,0},{3,1},{4,6},{5,7},{6,4},{7,5},{8,10},{9,11},{10,... | collective-permute-start | bytes 311048 | tf_op jit(solution)/shard_map/ppermute | solution.py:166
  20.1 6.0 %collective-permute-start.8 = (bf16[36,1440]{1,0:T(8,128)(2,1)S(1)}, bf16[36,1440]{1,0:T(8,128)(2,1)S(1)}, u32[]{:S(2)}, u32[]{:S(2)}) collective-permute-start(bf16[36,1440]{1,0:T(8,128)(2,1)S(1)} %collective-permute-done.7.rest_6_), channel_id=1, source_target_pairs={{0,4},{1,5},{2,6},{3,7},{4,0},{5,1},{6,2},{7,3},{8,12},{9,13},{10,... | collective-permute-start | bytes 311048 | tf_op jit(solution)/shard_map/ppermute | solution.py:166
  23.8 4.7 %collective-permute-start.15 = (bf16[36,1440]{1,0:T(8,128)(2,1)S(1)}, bf16[36,1440]{1,0:T(8,128)(2,1)S(1)}, u32[]{:S(2)}, u32[]{:S(2)}) collective-permute-start(bf16[36,1440]{1,0:T(8,128)(2,1)S(1)} %collective-permute-done.7.rest_6_), channel_id=1, source_target_pairs={{0,2},{1,3},{2,0},{3,1},{4,6},{5,7},{6,4},{7,5},{8,10},{9,11},{10,... | collective-permute-start | bytes 311048 | tf_op jit(solution)/shard_map/ppermute | solution.py:166
  23.8 4.7 %collective-permute-start.14 = (bf16[36,1440]{1,0:T(8,128)(2,1)S(1)}, bf16[36,1440]{1,0:T(8,128)(2,1)S(1)}, u32[]{:S(2)}, u32[]{:S(2)}) collective-permute-start(bf16[36,1440]{1,0:T(8,128)(2,1)S(1)} %collective-permute-done.6.rest_5_), channel_id=1, source_target_pairs={{0,2},{1,3},{2,0},{3,1},{4,6},{5,7},{6,4},{7,5},{8,10},{9,11},{10,... | collective-permute-start | bytes 311048 | tf_op jit(solution)/shard_map/ppermute | solution.py:166
  24.3 4.2 %collective-permute-start.12 = (bf16[36,1440]{1,0:T(8,128)(2,1)S(1)}, bf16[36,1440]{1,0:T(8,128)(2,1)S(1)}, u32[]{:S(2)}, u32[]{:S(2)}) collective-permute-start(bf16[36,1440]{1,0:T(8,128)(2,1)S(1)} %collective-permute-done.4.rest_3_), channel_id=1, source_target_pairs={{0,2},{1,3},{2,0},{3,1},{4,6},{5,7},{6,4},{7,5},{8,10},{9,11},{10,... | collective-permute-start | bytes 311048 | tf_op jit(solution)/shard_map/ppermute | solution.py:166
  33.3 3.5 %collective-permute-start.18 = (bf16[8,36,864]{2,0,1:T(8,128)(2,1)S(1)}, bf16[8,36,864]{2,0,1:T(8,128)(2,1)S(1)}, u32[]{:S(2)}, u32[]{:S(2)}) collective-permute-start(bf16[8,36,864]{2,0,1:T(8,128)(2,1)S(1)} %copy.11), channel_id=1, source_target_pairs={{0,2},{1,3},{2,0},{3,1},{4,6},{5,7},{6,4},{7,5},{8,10},{9,11},{10,... | collective-permute-start | bytes 1493000 | tf_op jit(solution)/shard_map/ppermute | solution.py:166
  35.1 19.6 %collective-permute-start.17 = (bf16[196,864]{1,0:T(8,128)(2,1)S(1)}, bf16[196,864]{1,0:T(8,128)(2,1)S(1)}, u32[]{:S(2)}, u32[]{:S(2)}) collective-permute-start(bf16[196,864]{1,0:T(8,128)(2,1)S(1)} %shard_map.107), channel_id=1, source_target_pairs={{0,1},{1,0},{2,3},{3,2},{4,5},{5,4},{6,7},{7,6},{8,9},{9,8},{10,11... | collective-permute-start | bytes 1016072 | tf_op jit(solution)/shard_map/ppermute | solution.py:166
  37.0 11.5 %collective-permute-start.19 = (bf16[2,36,864]{2,1,0:T(8,128)(2,1)S(1)}, bf16[2,36,864]{2,1,0:T(8,128)(2,1)S(1)}, u32[]{:S(2)}, u32[]{:S(2)}) collective-permute-start(bf16[2,36,864]{2,1,0:T(8,128)(2,1)S(1)} %get-tuple-element.48), channel_id=1, source_target_pairs={{0,4},{1,5},{2,6},{3,7},{4,0},{5,1},{6,2},{7,3},{8,12},{9,13},{10,... | collective-permute-start | bytes 373256 | tf_op jit(solution)/shard_map/ppermute | solution.py:166
  38.5 6.2 %collective-permute-start.21 = (bf16[36,864]{1,0:T(8,128)(2,1)S(1)}, bf16[36,864]{1,0:T(8,128)(2,1)S(1)}, u32[]{:S(2)}, u32[]{:S(2)}) collective-permute-start(bf16[36,864]{1,0:T(8,128)(2,1)S(1)} %get-tuple-element.51), channel_id=1, source_target_pairs={{0,4},{1,5},{2,6},{3,7},{4,0},{5,1},{6,2},{7,3},{8,12},{9,13},{10,... | collective-permute-start | bytes 186632 | tf_op jit(solution)/shard_map/ppermute | solution.py:166
  39.1 9.3 %collective-permute-start.23 = (bf16[36,864]{1,0:T(8,128)(2,1)S(1)}, bf16[36,864]{1,0:T(8,128)(2,1)S(1)}, u32[]{:S(2)}, u32[]{:S(2)}) collective-permute-start(bf16[36,864]{1,0:T(8,128)(2,1)S(1)} %get-tuple-element.52), channel_id=1, source_target_pairs={{0,4},{1,5},{2,6},{3,7},{4,0},{5,1},{6,2},{7,3},{8,12},{9,13},{10,... | collective-permute-start | bytes 186632 | tf_op jit(solution)/shard_map/ppermute | solution.py:166
  44.8 7.0 %collective-permute-start.22 = (bf16[36,864]{1,0:T(8,128)(2,1)S(1)}, bf16[36,864]{1,0:T(8,128)(2,1)S(1)}, u32[]{:S(2)}, u32[]{:S(2)}) collective-permute-start(bf16[36,864]{1,0:T(8,128)(2,1)S(1)} %shard_map.112), channel_id=1, source_target_pairs={{0,24},{1,25},{2,26},{3,27},{4,28},{5,29},{6,30},{7,31},{8,16},{9,... | collective-permute-start | bytes 186632 | tf_op jit(solution)/shard_map/ppermute | solution.py:166
  48.4 5.3 %collective-permute-start.24 = (bf16[36,864]{1,0:T(8,128)(2,1)S(1)}, bf16[36,864]{1,0:T(8,128)(2,1)S(1)}, u32[]{:S(2)}, u32[]{:S(2)}) collective-permute-start(bf16[36,864]{1,0:T(8,128)(2,1)S(1)} %shard_map.113), channel_id=1, source_target_pairs={{0,16},{1,17},{2,18},{3,19},{4,20},{5,21},{6,22},{7,23},{8,24},{9,... | collective-permute-start | bytes 186632 | tf_op jit(solution)/shard_map/ppermute | solution.py:166
  48.5 5.2 %collective-permute-start.20 = (bf16[36,864]{1,0:T(8,128)(2,1)S(1)}, bf16[36,864]{1,0:T(8,128)(2,1)S(1)}, u32[]{:S(2)}, u32[]{:S(2)}) collective-permute-start(bf16[36,864]{1,0:T(8,128)(2,1)S(1)} %get-tuple-element.50), channel_id=1, source_target_pairs={{0,8},{1,9},{2,10},{3,11},{4,12},{5,13},{6,14},{7,15},{8,0},{9,1},... | collective-permute-start | bytes 186632 | tf_op jit(solution)/shard_map/ppermute | solution.py:166
  53.8 4.0 %collective-permute-start.25 = (bf16[36,288]{1,0:T(8,128)(2,1)S(1)}, bf16[36,288]{1,0:T(8,128)(2,1)S(1)}, u32[]{:S(2)}, u32[]{:S(2)}) collective-permute-start(bf16[36,288]{1,0:T(8,128)(2,1)S(1)} %get-tuple-element.53), channel_id=1, source_target_pairs={{0,1},{1,0},{2,3},{3,2},{4,5},{5,4},{6,7},{7,6},{8,9},{9,8},{10,11... | collective-permute-start | bytes 62216 | tf_op jit(solution)/shard_map/ppermute | solution.py:166
  (8 other events, 53.1 us)

commit v2 on v1

--- a/solution.py
+++ b/solution.py
@@ -158,6 +158,8 @@
 KLANES = HERE * KEYS
 QKV = 3 * HALF
 SHARD = QKV + D
+LOW = 512
+EARLY = 11
 SEND = D + HALF
 BF16, F32 = jnp.bfloat16, jnp.float32
 
@@ -261,22 +263,57 @@
     return (lane >= h * HEAD) & (lane < (h + 1) * HEAD)
 
 
+def pre_kernel(rel_ref, pool_ref, order_ref, *rest):
+    blocks, (w_ref, q_ref, kv_ref, sel_ref) = rest[:EARLY], rest[EARLY:]
+    for s in range(EARLY):
+        at = s * SLOT
+        if s < EARLY - 1:
+            w_ref[at + 32 : at + SLOT, :] = jnp.zeros((16, SHARD), BF16)
+            w_ref[at : at + ROWS, :] = blocks[s][...]
+        else:
+            w_ref[at:LOW, :] = blocks[s][: LOW - at, :]
+    q_ref[...] = dot(rel_ref[:, :LOW], w_ref[:, :HALF])
+    kv_ref[...] = dot(pool_ref[:, :LOW], w_ref[:, 256:QKV])
+    first = pl.multiple_of(lax.axis_index("seq") * HALF, HALF)
+    sel_ref[...] = dot(order_ref[pl.ds(first, HALF), :LOW], w_ref[:, QKV:])
+
+
+def weight_grads(half, grad_scale, relt_ref, poolt_ref, dq_ref, e_ref, g_ref, out_ref):
+    rows = slice(half * 8 * SLOT, (half + 1) * 8 * SLOT)
+    g_q = dot(relt_ref[0, rows, :], dq_ref[:FSLOT, :]) + dot(relt_ref[1, rows, :], dq_ref[FSLOT:, :])
+    g_kv = dot(poolt_ref[rows, :], e_ref[...]) * 4.0
+    g_ref[:, :256] = g_q[:, :256] * grad_scale
+    g_ref[:, 256:384] = (g_q[:, 256:] + g_kv[:, :128]) * grad_scale
+    g_ref[:, 384:] = g_kv[:, 128:] * grad_scale
+    for s in range(8):
+        out_ref[s] = g_ref[s * SLOT : s * SLOT + ROWS, :].astype(BF16)
+
+
+def own_kernel(grad_scale, relt_ref, poolt_ref, dq_ref, e_ref, out_ref, g_ref):
+    weight_grads(0, grad_scale, relt_ref, poolt_ref, dq_ref, e_ref, g_ref, out_ref)
+
+
 def main_kernel(grad_scale, valid_ref, rel_ref, relt_ref, pool_ref, poolt_ref, order_ref, down_ref, dpeer_ref, *rest):
-    blocks = rest[:16]
-    gown_ref, goth_ref, w_ref, dq_ref, e_ref, mixed_ref, outh_ref = rest[16:23]
-    cot_ref, kbig_ref, vbig_ref, s_ref, p_ref, ds_ref, g_ref = rest[23:]
+    q_ref, kv_ref, sel_ref = rest[:3]
+    blocks, rest = rest[3 : 20 - EARLY], rest[20 - EARLY :]
+    goth_ref, w_ref, dq_ref, e_ref, mixed_ref, outh_ref = rest[:6]
+    cot_ref, kbig_ref, vbig_ref, s_ref, p_ref, ds_ref, g_ref = rest[6:]
     y = lax.axis_index("seq")
     scale = 1.0 / math.sqrt(HEAD)
-    for s in range(16):
-        w_ref[s * SLOT + 32 : (s + 1) * SLOT, :] = jnp.zeros((16, SHARD), BF16)
-        w_ref[s * SLOT : s * SLOT + ROWS, :] = blocks[s][...]
+    straddle = LOW - (EARLY - 1) * SLOT
+    w_ref[:16, :] = jnp.zeros((16, SHARD), BF16)
+    w_ref[: ROWS - straddle, :] = blocks[0][straddle:, :]
+    for s in range(EARLY, 16):
+        at = s * SLOT - LOW
+        w_ref[at + 32 : at + SLOT, :] = jnp.zeros((16, SHARD), BF16)
+        w_ref[at : at + ROWS, :] = blocks[s - EARLY + 1][...]
     for f, src in enumerate((down_ref, dpeer_ref)):
         at = f * FSLOT
         cot_ref[at + 192 : at + FSLOT, :] = jnp.zeros((16, D), BF16)
         cot_ref[at : at + FRAME_TOK, :] = src[...]
 
-    queries = dot(rel_ref[...], w_ref[:, :HALF]).astype(BF16)
-    kv = dot(pool_ref[...], w_ref[:, 256:QKV])
+    queries = (q_ref[...] + dot(rel_ref[:, LOW:], w_ref[:, :HALF])).astype(BF16)
+    kv = kv_ref[...] + dot(pool_ref[:, LOW:], w_ref[:, 256:QKV])
     kv = kv[:KEYS] + kv[KEYS:]
     keys = kv[:, 32 : 32 + HALF].astype(BF16)
     values = kv[:, 32 + HALF :].astype(BF16)
@@ -284,8 +321,8 @@
         lanes = head_lanes(h)
         kbig_ref[h * KEYS : (h + 1) * KEYS, :] = jnp.where(lanes, keys, BF16(0))
         vbig_ref[h * KEYS : (h + 1) * KEYS, :] = jnp.where(lanes, values, BF16(0))
-    select = order_ref[pl.ds(pl.multiple_of(y * HALF, HALF), HALF), :]
-    outh_ref[...] = dot(select, w_ref[:, QKV:]).astype(BF16)
+    select = order_ref[pl.ds(pl.multiple_of(y * HALF, HALF), HALF), LOW:]
+    outh_ref[...] = (sel_ref[...] + dot(select, w_ref[:, QKV:])).astype(BF16)
     d_mixed = dot(cot_ref[...], outh_ref[...], NT).astype(BF16)
 
     s_ref[...] = dot(queries, kbig_ref[...], NT)
@@ -321,46 +358,39 @@
     e = jnp.concatenate([jnp.zeros((KEYS, 32), F32), d_keys, d_values], axis=1).astype(BF16)
     e_ref[:KEYS, :] = e
     e_ref[KEYS:, :] = e
-    dq = dq_ref[...]
-    g_q = dot(relt_ref[0], dq[:FSLOT]) + dot(relt_ref[1], dq[FSLOT:])
-    g_kv = dot(poolt_ref[...], e_ref[...]) * 4.0
-    g_ref[:, :256] = g_q[:, :256] * grad_scale
-    g_ref[:, 256:384] = (g_q[:, 256:] + g_kv[:, :128]) * grad_scale
-    g_ref[:, 384:] = g_kv[:, 128:] * grad_scale
-    for s in range(8):
-        gown_ref[s] = g_ref[s * SLOT : s * SLOT + ROWS, :].astype(BF16)
-        goth_ref[s] = g_ref[(s + 8) * SLOT : (s + 8) * SLOT + ROWS, :].astype(BF16)
-
-
-def d_normed_of(f, w_ref, dq_ref, e_ref):
+    weight_grads(1, grad_scale, relt_ref, poolt_ref, dq_ref, e_ref, g_ref, goth_ref)
+
+
+def d_normed_of(f, low_ref, high_ref, dq_ref, e_ref):
     rows = slice(f * FSLOT, (f + 1) * FSLOT)
     keys = key_of_token((TOK2, 1), 0)[rows]
     d_tokens = dot(one_hot(keys == iota((FSLOT, KEYS), 1)), e_ref[:KEYS, :]).astype(BF16)
-    return dot(dq_ref[rows, :], w_ref[:, :384], NT) + dot(d_tokens, w_ref[:, 256:QKV], NT)
-
-
-def cross_kernel(w_ref, dq_ref, e_ref, mixed_ref, order_ref, send_ref):
-    peer = dot(d_normed_of(1, w_ref, dq_ref, e_ref).astype(BF16), order_ref[...], NT)
+    d_queries = dq_ref[rows, :]
+    return jnp.concatenate(
+        [dot(d_queries, w[:, :384], NT) + dot(d_tokens, w[:, 256:QKV], NT) for w in (low_ref, high_ref)], axis=1
+    )
+
+
+def cross_kernel(low_ref, high_ref, dq_ref, e_ref, mixed_ref, order_ref, send_ref):
+    peer = dot(d_normed_of(1, low_ref, high_ref, dq_ref, e_ref).astype(BF16), order_ref[...], NT)
     send_ref[:, :D] = peer[:FRAME_TOK].astype(BF16)
     send_ref[:, D:] = mixed_ref[FSLOT : FSLOT + FRAME_TOK, :]
 
 
-def late_kernel(w_ref, dq_ref, e_ref, order_ref, nat_ref, oth_ref):
+def late_kernel(low_ref, high_ref, dq_ref, e_ref, order_ref, nat_ref, oth_ref):
     order = order_ref[...]
-    own = d_normed_of(0, w_ref, dq_ref, e_ref)
-    hi = own.astype(BF16)
-    lo = (own - hi.astype(F32)).astype(BF16)
-    nat_ref[...] = (dot(hi, order, NT) + dot(lo, order, NT))[:FRAME_TOK]
+    own = d_normed_of(0, low_ref, high_ref, dq_ref, e_ref).astype(BF16)
+    nat_ref[...] = dot(own, order, NT)[:FRAME_TOK].astype(BF16)
     other = 1 - lax.axis_index("seq")
     select = order_ref[pl.ds(pl.multiple_of(other * HALF, HALF), HALF), :]
-    oth_ref[...] = dot(select, w_ref[:, QKV:]).astype(BF16)
+    oth_ref[...] = (dot(select[:, :LOW], low_ref[:, QKV:]) + dot(select[:, LOW:], high_ref[:, QKV:])).astype(BF16)
 
 
 def last_kernel(yone_ref, second_ref, dtwo_ref, gain_ref, got_ref, dn_ref, mixed_ref, outh_ref, oth_ref, x_ref, dx_ref):
     branch = dot(mixed_ref[:FRAME_TOK, :], outh_ref[...]) + dot(got_ref[:, D:], oth_ref[...])
     x_ref[...] = (yone_ref[...].astype(F32) - branch).astype(BF16)
     xhat, inverse = standardize(second_ref[...].astype(F32))
-    gained = (dn_ref[...] + got_ref[:, :D].astype(F32)) * gain_ref[...].reshape(1, D)
+    gained = (dn_ref[...].astype(F32) + got_ref[:, :D].astype(F32)) * gain_ref[...].reshape(1, D)
     lower = inverse * (
         gained
         - jnp.mean(gained, axis=-1, keepdims=True)
@@ -401,14 +431,28 @@
     sum_ref[...] = (kept_ref[at].astype(F32) + got_ref[...].astype(F32)).astype(BF16)
 
 
+def part_kernel(at, kept_ref, got_ref, cross_ref, stay_ref):
+    store_parts(kept_ref[at].astype(F32) + got_ref[...].astype(F32), cross_ref, stay_ref)
+
+
 def near_kernel(kept_ref, got_ref, a_ref, o_ref):
     a_ref[...] = (kept_ref[1].astype(F32) + got_ref[0].astype(F32)).astype(BF16)
     o_ref[...] = kept_ref[0].astype(F32) + got_ref[1].astype(F32)
 
 
 def sum_kernel(o_ref, a_ref, ab_ref, b_ref, cross_ref, stay_ref):
-    total = o_ref[...] + a_ref[...].astype(F32) + ab_ref[...].astype(F32) + b_ref[...].astype(F32)
-    store_parts(total, cross_ref, stay_ref)
+    total = o_ref[...] + a_ref[...].astype(F32) + ab_ref[...].astype(F32)
+    y = lax.axis_index("seq")
+
+    @pl.when(y == 0)
+    def _():
+        cross_ref[...] = (total[:, 2 * HALF :] + b_ref[...].astype(F32)).astype(BF16)
+        stay_ref[...] = total[:, : 2 * HALF]
+
+    @pl.when(y == 1)
+    def _():
+        cross_ref[...] = (total[:, :HALF] + b_ref[...].astype(F32)).astype(BF16)
+        stay_ref[...] = total[:, HALF:]
 
 
 def join_kernel(crossed_ref, *refs):
@@ -477,18 +521,30 @@
         flops=1_200_000_000,
         moved=3_000_000,
     )
-    g_own, g_oth, w_rel, d_q, e, mixed, out_own = call(
+    blocks = mine + other
+    w_low, q_low, kv_low, sel_low = call(
+        pre_kernel,
+        (
+            shape(LOW, SHARD),
+            shape(TOK2, HALF, kind=F32),
+            shape(2 * KEYS, 608, kind=F32),
+            shape(HALF, D, kind=F32),
+        ),
+        (rel, pool, order) + blocks[:EARLY],
+        flops=800_000_000,
+        moved=4_000_000,
+    )
+    g_oth, w_high, d_q, e, mixed, out_own = call(
         functools.partial(main_kernel, grad_scale),
         (
             shape(8, ROWS, QKV),
-            shape(8, ROWS, QKV),
-            shape(REL, SHARD),
+            shape(REL - LOW, SHARD),
             shape(TOK2, 384),
             shape(2 * KEYS, 608),
             shape(TOK2, HALF),
             shape(HALF, D),
         ),
-        (frames_valid, rel, rel_t, pool, pool_t, order, cot, cot_peer) + mine + other,
+        (frames_valid, rel, rel_t, pool, pool_t, order, cot, cot_peer, q_low, kv_low, sel_low) + blocks[EARLY - 1 :],
         scratch=(
             pltpu.VMEM((TOK2, D), BF16),
             pltpu.VMEM((KLANES, HALF), BF16),
@@ -496,7 +552,7 @@
             pltpu.VMEM((TOK2, KLANES), F32),
             pltpu.VMEM((TOK2, KLANES), BF16),
             pltpu.VMEM((TOK2, KLANES), BF16),
-            pltpu.VMEM((REL, QKV), F32),
+            pltpu.VMEM((8 * SLOT, QKV), F32),
         ),
         smem=1,
         flops=4_000_000_000,
@@ -504,6 +560,14 @@
         limit=32 << 10,
     )
 
+    g_own = call(
+        functools.partial(own_kernel, grad_scale),
+        shape(8, ROWS, QKV),
+        (rel_t, pool_t, d_q, e),
+        scratch=(pltpu.VMEM((8 * SLOT, QKV), F32),),
+        flops=500_000_000,
+        moved=2_000_000,
+    )
     block, pair = shape(ROWS, QKV), shape(2, ROWS, QKV)
     wide = shape(ROWS, QKV, kind=F32)
     kept, x_ab, x_b, near = call(
@@ -514,10 +578,15 @@
     )
     got_ab, got_b = swap(x_ab, OVER_X), swap(x_b, OVER_X)
     to_ab = call(functools.partial(add_kernel, 3), block, (kept, got_ab), moved=200_000)
-    to_b = call(functools.partial(add_kernel, 2), block, (kept, got_b), moved=200_000)
+    to_b = call(
+        functools.partial(part_kernel, 2),
+        (shape(ROWS, HALF), shape(ROWS, 2 * HALF)),
+        (kept, got_b),
+        moved=200_000,
+    )
     to_a, here = call(near_kernel, (block, wide), (kept, swap(near, OVER_X)), moved=400_000)
     from_ab = swap(to_ab, OVER_Z1 | OVER_Z2)
-    from_b = swap(to_b, OVER_Z2)
+    from_b, from_b_stay = swap(to_b[0], OVER_Z2), swap(to_b[1], OVER_Z2)
     from_a = swap(to_a, OVER_Z1)
     crossing, stay = call(
         sum_kernel,
@@ -526,20 +595,20 @@
         moved=400_000,
     )
     crossed = swap(crossing, OVER_Y)
-    grad_qkv = call(join_kernel, wide, (crossed, stay), moved=300_000)
+    grad_qkv = call(join_kernel, wide, (crossed, stay, from_b_stay), moved=300_000)
 
     send = call(
         cross_kernel,
         shape(FRAME_TOK, SEND),
-        (w_rel, d_q, e, mixed, order),
+        (w_low, w_high, d_q, e, mixed, order),
         flops=600_000_000,
         moved=4_000_000,
     )
     got = swap(send, OVER_Y)
     d_normed, out_oth = call(
         late_kernel,
-        (shape(FRAME_TOK, D, kind=F32), shape(HALF, D)),
-        (w_rel, d_q, e, order),
+        (shape(FRAME_TOK, D), shape(HALF, D)),
+        (w_low, w_high, d_q, e, order),
         flops=1_000_000_000,
         moved=3_000_000,
     )

time: 58.7 us -> 60.3 us (1.027)
  starting transfers between devices: 26.9 us -> 28.3 us
    ppermute x26 -> x27, starting transfers between devices: 26.9 us -> 28.3 us  [swap(): return lax.ppermute(array, AXES, [(i, i ^ mask) for i in range(32)])]
    ppermute x26 -> x27, waiting for transfers between devices: 13.7 us -> 13.9 us  [swap(): return lax.ppermute(array, AXES, [(i, i ^ mask) for i in range(32)])]
    pallas_call x13 -> x15, Pallas kernels: 14.6 us -> 14.6 us  [call(): pl.pallas_call(kernel, out_shape=outs, in_specs=[pl.BlockSpec(memory_spac...]
  transfers between devices with their start and end apart: 26 -> 27, of which waited for: 8 -> 8; matrix products, arithmetic and copies ran while one was open for 0% -> 0% of each run, Pallas kernels for 13% -> 14%
where the time goes in v2:
time: 60.3 us; the launch traced here: 60.1 us
  starting transfers between devices  28.3 us (47%)
  Pallas kernels  14.6 us (24%)
  waiting for transfers between devices  13.9 us (23%)
  local copies, waits for them, and re-layouts  1.77 us (3%)
  between operations  1.51 us (3%)
    ppermute x27, starting transfers between devices, swap(): return lax.ppermute(array, AXES, [(i, i ^ mask) for i in range(32)])  28.3 us
    pallas_call x15, Pallas kernels, call(): pl.pallas_call(kernel, out_shape=outs, in_specs=[pl.BlockSpec(memory_spac...  14.6 us
    ppermute x27, waiting for transfers between devices, swap(): return lax.ppermute(array, AXES, [(i, i ^ mask) for i in range(32)])  13.9 us
    unnamed x12, local copies, waits for them, and re-layouts  1.65 us
  transfers between devices with their start and end apart: 27, of which 8 were waited for; matrix products, arithmetic and copies ran while one was open for 0% of the time, Pallas kernels for 14%

profile of v2, /device:TPU:0, one launch (start us, length us, event | category | flops | bytes accessed | tf_op | source)
XLA Modules:
  0.0 60.1 jit_solution(4424156215955770054)
XLA Ops:
  0.6 1.7 %shard_map.105.rest_0_ = bf16[36,1440]{1,0:T(8,128)(2,1)} custom-call(bf16[36,1728]{1,0:T(8,128)(2,1)} %qkv_hbm.1, bf16[36,576]{1,0:T(8,128)(2,1)} %out_hbm.1), custom_call_target="tpu_custom_call" | custom-call | bytes 400000 | tf_op jit(solution)/shard_map/pallas_call | solution.py:473
  2.4 4.1 %collective-permute-start.4 = (bf16[36,1440]{1,0:T(8,128)(2,1)}, bf16[36,1440]{1,0:T(8,128)(2,1)S(1)}, u32[]{:S(2)}, u32[]{:S(2)}) collective-permute-start(bf16[36,1440]{1,0:T(8,128)(2,1)} %shard_map.105.rest_0_), channel_id=1, source_target_pairs={{0,16},{1,17},{2,18},{3,19},{4,20},{5,21},{6,22},{7,23},{8,24},{9,... | collective-permute-start | bytes 311048 | tf_op jit(solution)/shard_map/ppermute | solution.py:168
  6.5 1.6 %collective-permute-start.2 = (bf16[36,1440]{1,0:T(8,128)(2,1)}, bf16[36,1440]{1,0:T(8,128)(2,1)S(1)}, u32[]{:S(2)}, u32[]{:S(2)}) collective-permute-start(bf16[36,1440]{1,0:T(8,128)(2,1)} %shard_map.105.rest_0_), channel_id=1, source_target_pairs={{0,8},{1,9},{2,10},{3,11},{4,12},{5,13},{6,14},{7,15},{8,0},{9,1},... | collective-permute-start | bytes 311048 | tf_op jit(solution)/shard_map/ppermute | solution.py:168
  8.1 1.5 %collective-permute-start.1 = (bf16[36,1440]{1,0:T(8,128)(2,1)}, bf16[36,1440]{1,0:T(8,128)(2,1)S(1)}, u32[]{:S(2)}, u32[]{:S(2)}) collective-permute-start(bf16[36,1440]{1,0:T(8,128)(2,1)} %shard_map.105.rest_0_), channel_id=1, source_target_pairs={{0,4},{1,5},{2,6},{3,7},{4,0},{5,1},{6,2},{7,3},{8,12},{9,13},{10,... | collective-permute-start | bytes 311048 | tf_op jit(solution)/shard_map/ppermute | solution.py:168
  9.6 1.5 %collective-permute-start = (bf16[196,576]{1,0:T(8,128)(2,1)}, bf16[196,576]{1,0:T(8,128)(2,1)S(1)}, u32[]{:S(2)}, u32[]{:S(2)}) collective-permute-start(bf16[196,576]{1,0:T(8,128)(2,1)} %bitcast.8), channel_id=1, source_target_pairs={{0,1},{1,0},{2,3},{3,2},{4,5},{5,4},{6,7},{7,6},{8,9},{9,8},{10,11... | collective-permute-start | bytes 677384 | tf_op jit(solution)/shard_map/ppermute | solution.py:168
  11.1 1.7 %collective-permute-done.4.rest_4_ = bf16[36,1440]{1,0:T(8,128)(2,1)S(1)} collective-permute-done((bf16[36,1440]{1,0:T(8,128)(2,1)}, bf16[36,1440]{1,0:T(8,128)(2,1)S(1)}, u32[]{:S(2)}, u32[]{:S(2)}) %collective-permute-start.4) | collective-permute-done | bytes 103712 | tf_op jit(solution)/shard_map/ppermute | solution.py:168
  13.9 1.5 %collective-permute-start.5 = (bf16[36,1440]{1,0:T(8,128)(2,1)S(1)}, bf16[36,1440]{1,0:T(8,128)(2,1)S(1)}, u32[]{:S(2)}, u32[]{:S(2)}) collective-permute-start(bf16[36,1440]{1,0:T(8,128)(2,1)S(1)} %collective-permute-done.4.rest_4_), channel_id=1, source_target_pairs={{0,4},{1,5},{2,6},{3,7},{4,0},{5,1},{6,2},{7,3},{8,12},{9,13},{10,... | collective-permute-start | bytes 311048 | tf_op jit(solution)/shard_map/ppermute | solution.py:168
  16.0 2.5 %collective-permute-done.6.rest_6_ = bf16[36,1440]{1,0:T(8,128)(2,1)S(1)} collective-permute-done((bf16[36,1440]{1,0:T(8,128)(2,1)S(1)}, bf16[36,1440]{1,0:T(8,128)(2,1)S(1)}, u32[]{:S(2)}, u32[]{:S(2)}) %collective-permute-start.6) | collective-permute-done | bytes 103712 | tf_op jit(solution)/shard_map/ppermute | solution.py:168
  19.4 2.2 %collective-permute-start.7 = (bf16[36,1440]{1,0:T(8,128)(2,1)S(1)}, bf16[36,1440]{1,0:T(8,128)(2,1)S(1)}, u32[]{:S(2)}, u32[]{:S(2)}) collective-permute-start(bf16[36,1440]{1,0:T(8,128)(2,1)S(1)} %collective-permute-done.6.rest_6_), channel_id=1, source_target_pairs={{0,4},{1,5},{2,6},{3,7},{4,0},{5,1},{6,2},{7,3},{8,12},{9,13},{10,... | collective-permute-start | bytes 311048 | tf_op jit(solution)/shard_map/ppermute | solution.py:168
  21.7 1.5 %collective-permute-start.11 = (bf16[196,576]{1,0:T(8,128)(2,1)}, bf16[196,576]{1,0:T(8,128)(2,1)S(1)}, u32[]{:S(2)}, u32[]{:S(2)}) collective-permute-start(bf16[196,576]{1,0:T(8,128)(2,1)} %bitcast.10), channel_id=1, source_target_pairs={{0,1},{1,0},{2,3},{3,2},{4,5},{5,4},{6,7},{7,6},{8,9},{9,8},{10,11... | collective-permute-start | bytes 677384 | tf_op jit(solution)/shard_map/ppermute | solution.py:168
  23.9 0.9 %copy-done.3 = bf16[1,196,576]{2,1,0:T(8,128)(2,1)S(1)} copy-done((bf16[1,196,576]{2,1,0:T(8,128)(2,1)S(1)}, bf16[1,196,576]{2,1,0:T(8,128)(2,1)}, u32[]{:S(2)}) %copy-start.3) | copy-done | bytes 225816
  26.6 2.4 %shard_map.104 = (bf16[416,768]{1,0:T(8,128)(2,1)S(1)}, bf16[2,768,208]{2,1,0:T(8,128)(2,1)S(1)}, bf16[256,768]{1,0:T(8,128)(2,1)S(1)}, bf16[768,256]{1,0:T(8,128)(2,1)S(1)}, bf16[576,768]{1,0:T(8,128)(2,1)S(1)}) custom-call(bf16[196,576]{1,0:T(8,128)(2,1)S(1)} %get-tuple-element.34.own_ref.second_ref, bf16[196,576]{1,0:T(8,128)(2,1)S(1)} %collective-permute-done.peer_ref, ...), custom_call_target="tpu_custom_call" | custom-call | flops 1200000000 | bytes 3000000 | tf_op jit(solution)/shard_map/pallas_call | solution.py:473
  30.1 3.4 %shard_map.107 = (bf16[8,36,864]{2,1,0:T(8,128)(2,1)S(1)}, bf16[256,1440]{1,0:T(8,128)(2,1)S(1)}, bf16[416,384]{1,0:T(8,128)(2,1)S(1)}, bf16[256,608]{1,0:T(8,12...) custom-call(s32[1]{0:T(128)S(6)} %copy.13.valid_ref, ...), custom_call_target="tpu_custom_call" | custom-call | flops 4000000000 | bytes 8000000 | tf_op jit(solution)/shard_map/pallas_call | solution.py:473
  33.7 1.3 %shard_map.108 = bf16[196,864]{1,0:T(8,128)(2,1)S(1)} custom-call(bf16[512,1440]{1,0:T(8,128)(2,1)S(1)} %get-tuple-element.39.low_ref, bf16[256,1440]{1,0:T(8,128)(2,1)S(1)} %get-tuple-element.45.high_ref, bf16[416,384]{1,0:T(8,128)(2,1)S(1)} %get-tuple-element.46.dq_ref, bf16[256,608]{1,0:T(8,128)(2,1)S(1)} %get-tuple-element.47.e_ref, ...), custom_call_target="tpu_custom_call" | custom-call | flops 600000000 | bytes 4000000 | tf_op jit(solution)/shard_map/pallas_call | solution.py:473
  36.4 1.5 %collective-permute-start.19 = (bf16[2,36,864]{2,1,0:T(8,128)(2,1)S(1)}, bf16[2,36,864]{2,1,0:T(8,128)(2,1)S(1)}, u32[]{:S(2)}, u32[]{:S(2)}) collective-permute-start(bf16[2,36,864]{2,1,0:T(8,128)(2,1)S(1)} %get-tuple-element.56), channel_id=1, source_target_pairs={{0,4},{1,5},{2,6},{3,7},{4,0},{5,1},{6,2},{7,3},{8,12},{9,13},{10,... | collective-permute-start | bytes 373256 | tf_op jit(solution)/shard_map/ppermute | solution.py:168
  38.5 1.4 %collective-permute-start.23 = (bf16[36,864]{1,0:T(8,128)(2,1)S(1)}, bf16[36,864]{1,0:T(8,128)(2,1)S(1)}, u32[]{:S(2)}, u32[]{:S(2)}) collective-permute-start(bf16[36,864]{1,0:T(8,128)(2,1)S(1)} %get-tuple-element.60), channel_id=1, source_target_pairs={{0,4},{1,5},{2,6},{3,7},{4,0},{5,1},{6,2},{7,3},{8,12},{9,13},{10,... | collective-permute-start | bytes 186632 | tf_op jit(solution)/shard_map/ppermute | solution.py:168
  39.8 4.7 %collective-permute-done.21.got_ref = bf16[36,864]{1,0:T(8,128)(2,1)S(1)} collective-permute-done((bf16[36,864]{1,0:T(8,128)(2,1)S(1)}, bf16[36,864]{1,0:T(8,128)(2,1)S(1)}, u32[]{:S(2)}, u32[]{:S(2)}) %collective-permute-start.21) | collective-permute-done | bytes 62240 | tf_op jit(solution)/shard_map/ppermute | solution.py:168
  44.6 3.1 %collective-permute-start.22 = (bf16[36,864]{1,0:T(8,128)(2,1)S(1)}, bf16[36,864]{1,0:T(8,128)(2,1)S(1)}, u32[]{:S(2)}, u32[]{:S(2)}) collective-permute-start(bf16[36,864]{1,0:T(8,128)(2,1)S(1)} %shard_map.114), channel_id=1, source_target_pairs={{0,24},{1,25},{2,26},{3,27},{4,28},{5,29},{6,30},{7,31},{8,16},{9,... | collective-permute-start | bytes 186632 | tf_op jit(solution)/shard_map/ppermute | solution.py:168
  48.3 2.4 %collective-permute-start.26 = (bf16[36,576]{1,0:T(8,128)(2,1)S(1)}, bf16[36,576]{1,0:T(8,128)(2,1)S(1)}, u32[]{:S(2)}, u32[]{:S(2)}) collective-permute-start(bf16[36,576]{1,0:T(8,128)(2,1)S(1)} %get-tuple-element.64), channel_id=1, source_target_pairs={{0,16},{1,17},{2,18},{3,19},{4,20},{5,21},{6,22},{7,23},{8,24},{9,... | collective-permute-start | bytes 124424 | tf_op jit(solution)/shard_map/ppermute | solution.py:168
  51.3 1.6 %shard_map.109 = (bf16[196,576]{1,0:T(8,128)(2,1)S(1)}, bf16[288,576]{1,0:T(8,128)(2,1)S(1)}) custom-call(bf16[512,1440]{1,0:T(8,128)(2,1)S(1)} %get-tuple-element.39.low_ref, bf16[256,1440]{1,0:T(8,128)(2,1)S(1)} %get-tuple-element.45.high_ref, bf16[416,384]{1,0:T(8,128)(2,1)S(1)} %get-tuple-element.46.dq_ref, ...), custom_call_target="tpu_custom_call" | custom-call | flops 1000000000 | bytes 3000000 | tf_op jit(solution)/shard_map/pallas_call | solution.py:473
  53.0 2.2 %collective-permute-done.20.a_ref = bf16[36,864]{1,0:T(8,128)(2,1)S(1)} collective-permute-done((bf16[36,864]{1,0:T(8,128)(2,1)S(1)}, bf16[36,864]{1,0:T(8,128)(2,1)S(1)}, u32[]{:S(2)}, u32[]{:S(2)}) %collective-permute-start.20) | collective-permute-done | bytes 62240 | tf_op jit(solution)/shard_map/ppermute | solution.py:168
  55.4 1.1 %collective-permute-start.25 = (bf16[36,288]{1,0:T(8,128)(2,1)S(1)}, bf16[36,288]{1,0:T(8,128)(2,1)S(1)}, u32[]{:S(2)}, u32[]{:S(2)}) collective-permute-start(bf16[36,288]{1,0:T(8,128)(2,1)S(1)} %get-tuple-element.62), channel_id=1, source_target_pairs={{0,1},{1,0},{2,3},{3,2},{4,5},{5,4},{6,7},{7,6},{8,9},{9,8},{10,11... | collective-permute-start | bytes 62216 | tf_op jit(solution)/shard_map/ppermute | solution.py:168
  56.5 1.4 %shard_map.110 = (bf16[196,576]{1,0:T(8,128)(2,1)}, bf16[196,576]{1,0:T(8,128)(2,1)}) custom-call(bf16[196,576]{1,0:T(8,128)(2,1)S(1)} %bitcast.6, bf16[196,576]{1,0:T(8,128)(2,1)S(1)} %get-tuple-element.34.own_ref.second_ref, bf16[196,576]{1,0:T(8,128)(2,1)S(1)} %bitcast.7, f32[576]{0:T(1024)S(1)} %get-tuple-element.35.gain_ref, ...), custom_call_target="tpu_custom_call" | custom-call | flops 300000000 | bytes 3000000 | tf_op jit(solution)/shard_map/pallas_call | solution.py:473
  57.9 1.4 %collective-permute-done.25.crossed_ref = bf16[36,288]{1,0:T(8,128)(2,1)S(1)} collective-permute-done((bf16[36,288]{1,0:T(8,128)(2,1)S(1)}, bf16[36,288]{1,0:T(8,128)(2,1)S(1)}, u32[]{:S(2)}, u32[]{:S(2)}) %collective-permute-start.25) | collective-permute-done | bytes 20768 | tf_op jit(solution)/shard_map/ppermute | solution.py:168
  (59 shorter events, 9.8 us)
Async XLA Ops:
  2.4 10.4 %collective-permute-start.4 = (bf16[36,1440]{1,0:T(8,128)(2,1)}, bf16[36,1440]{1,0:T(8,128)(2,1)S(1)}, u32[]{:S(2)}, u32[]{:S(2)}) collective-permute-start(bf16[36,1440]{1,0:T(8,128)(2,1)} %shard_map.105.rest_0_), channel_id=1, source_target_pairs={{0,16},{1,17},{2,18},{3,19},{4,20},{5,21},{6,22},{7,23},{8,24},{9,... | collective-permute-start | bytes 311048 | tf_op jit(solution)/shard_map/ppermute | solution.py:168
  6.5 6.3 %collective-permute-start.8 = (bf16[36,1440]{1,0:T(8,128)(2,1)}, bf16[36,1440]{1,0:T(8,128)(2,1)S(1)}, u32[]{:S(2)}, u32[]{:S(2)}) collective-permute-start(bf16[36,1440]{1,0:T(8,128)(2,1)} %shard_map.105.rest_0_), channel_id=1, source_target_pairs={{0,2},{1,3},{2,0},{3,1},{4,6},{5,7},{6,4},{7,5},{8,10},{9,11},{10,... | collective-permute-start | bytes 311048 | tf_op jit(solution)/shard_map/ppermute | solution.py:168
  6.5 7.4 %collective-permute-start.2 = (bf16[36,1440]{1,0:T(8,128)(2,1)}, bf16[36,1440]{1,0:T(8,128)(2,1)S(1)}, u32[]{:S(2)}, u32[]{:S(2)}) collective-permute-start(bf16[36,1440]{1,0:T(8,128)(2,1)} %shard_map.105.rest_0_), channel_id=1, source_target_pairs={{0,8},{1,9},{2,10},{3,11},{4,12},{5,13},{6,14},{7,15},{8,0},{9,1},... | collective-permute-start | bytes 311048 | tf_op jit(solution)/shard_map/ppermute | solution.py:168
  8.1 7.4 %collective-permute-start.1 = (bf16[36,1440]{1,0:T(8,128)(2,1)}, bf16[36,1440]{1,0:T(8,128)(2,1)S(1)}, u32[]{:S(2)}, u32[]{:S(2)}) collective-permute-start(bf16[36,1440]{1,0:T(8,128)(2,1)} %shard_map.105.rest_0_), channel_id=1, source_target_pairs={{0,4},{1,5},{2,6},{3,7},{4,0},{5,1},{6,2},{7,3},{8,12},{9,13},{10,... | collective-permute-start | bytes 311048 | tf_op jit(solution)/shard_map/ppermute | solution.py:168
  9.6 16.5 %collective-permute-start = (bf16[196,576]{1,0:T(8,128)(2,1)}, bf16[196,576]{1,0:T(8,128)(2,1)S(1)}, u32[]{:S(2)}, u32[]{:S(2)}) collective-permute-start(bf16[196,576]{1,0:T(8,128)(2,1)} %bitcast.8), channel_id=1, source_target_pairs={{0,1},{1,0},{2,3},{3,2},{4,5},{5,4},{6,7},{7,6},{8,9},{9,8},{10,11... | collective-permute-start | bytes 677384 | tf_op jit(solution)/shard_map/ppermute | solution.py:168
  12.8 5.7 %collective-permute-start.6 = (bf16[36,1440]{1,0:T(8,128)(2,1)S(1)}, bf16[36,1440]{1,0:T(8,128)(2,1)S(1)}, u32[]{:S(2)}, u32[]{:S(2)}) collective-permute-start(bf16[36,1440]{1,0:T(8,128)(2,1)S(1)} %collective-permute-done.4.rest_4_), channel_id=1, source_target_pairs={{0,8},{1,9},{2,10},{3,11},{4,12},{5,13},{6,14},{7,15},{8,0},{9,1},... | collective-permute-start | bytes 311048 | tf_op jit(solution)/shard_map/ppermute | solution.py:168
  13.9 5.5 %collective-permute-start.5 = (bf16[36,1440]{1,0:T(8,128)(2,1)S(1)}, bf16[36,1440]{1,0:T(8,128)(2,1)S(1)}, u32[]{:S(2)}, u32[]{:S(2)}) collective-permute-start(bf16[36,1440]{1,0:T(8,128)(2,1)S(1)} %collective-permute-done.4.rest_4_), channel_id=1, source_target_pairs={{0,4},{1,5},{2,6},{3,7},{4,0},{5,1},{6,2},{7,3},{8,12},{9,13},{10,... | collective-permute-start | bytes 311048 | tf_op jit(solution)/shard_map/ppermute | solution.py:168
  15.5 6.2 %collective-permute-start.10 = (bf16[36,1440]{1,0:T(8,128)(2,1)S(1)}, bf16[36,1440]{1,0:T(8,128)(2,1)S(1)}, u32[]{:S(2)}, u32[]{:S(2)}) collective-permute-start(bf16[36,1440]{1,0:T(8,128)(2,1)S(1)} %collective-permute-done.2.rest_2_), channel_id=1, source_target_pairs={{0,2},{1,3},{2,0},{3,1},{4,6},{5,7},{6,4},{7,5},{8,10},{9,11},{10,... | collective-permute-start | bytes 311048 | tf_op jit(solution)/shard_map/ppermute | solution.py:168
  15.5 10.0 %collective-permute-start.3 = (bf16[36,1440]{1,0:T(8,128)(2,1)S(1)}, bf16[36,1440]{1,0:T(8,128)(2,1)S(1)}, u32[]{:S(2)}, u32[]{:S(2)}) collective-permute-start(bf16[36,1440]{1,0:T(8,128)(2,1)S(1)} %collective-permute-done.2.rest_2_), channel_id=1, source_target_pairs={{0,4},{1,5},{2,6},{3,7},{4,0},{5,1},{6,2},{7,3},{8,12},{9,13},{10,... | collective-permute-start | bytes 311048 | tf_op jit(solution)/shard_map/ppermute | solution.py:168
  18.5 7.1 %collective-permute-start.9 = (bf16[36,1440]{1,0:T(8,128)(2,1)S(1)}, bf16[36,1440]{1,0:T(8,128)(2,1)S(1)}, u32[]{:S(2)}, u32[]{:S(2)}) collective-permute-start(bf16[36,1440]{1,0:T(8,128)(2,1)S(1)} %collective-permute-done.1.rest_1_), channel_id=1, source_target_pairs={{0,2},{1,3},{2,0},{3,1},{4,6},{5,7},{6,4},{7,5},{8,10},{9,11},{10,... | collective-permute-start | bytes 311048 | tf_op jit(solution)/shard_map/ppermute | solution.py:168
  19.4 6.8 %collective-permute-start.7 = (bf16[36,1440]{1,0:T(8,128)(2,1)S(1)}, bf16[36,1440]{1,0:T(8,128)(2,1)S(1)}, u32[]{:S(2)}, u32[]{:S(2)}) collective-permute-start(bf16[36,1440]{1,0:T(8,128)(2,1)S(1)} %collective-permute-done.6.rest_6_), channel_id=1, source_target_pairs={{0,4},{1,5},{2,6},{3,7},{4,0},{5,1},{6,2},{7,3},{8,12},{9,13},{10,... | collective-permute-start | bytes 311048 | tf_op jit(solution)/shard_map/ppermute | solution.py:168
  21.7 8.3 %collective-permute-start.11 = (bf16[196,576]{1,0:T(8,128)(2,1)}, bf16[196,576]{1,0:T(8,128)(2,1)S(1)}, u32[]{:S(2)}, u32[]{:S(2)}) collective-permute-start(bf16[196,576]{1,0:T(8,128)(2,1)} %bitcast.10), channel_id=1, source_target_pairs={{0,1},{1,0},{2,3},{3,2},{4,5},{5,4},{6,7},{7,6},{8,9},{9,8},{10,11... | collective-permute-start | bytes 677384 | tf_op jit(solution)/shard_map/ppermute | solution.py:168
  25.5 4.5 %collective-permute-start.15 = (bf16[36,1440]{1,0:T(8,128)(2,1)S(1)}, bf16[36,1440]{1,0:T(8,128)(2,1)S(1)}, u32[]{:S(2)}, u32[]{:S(2)}) collective-permute-start(bf16[36,1440]{1,0:T(8,128)(2,1)S(1)} %collective-permute-done.6.rest_6_), channel_id=1, source_target_pairs={{0,2},{1,3},{2,0},{3,1},{4,6},{5,7},{6,4},{7,5},{8,10},{9,11},{10,... | collective-permute-start | bytes 311048 | tf_op jit(solution)/shard_map/ppermute | solution.py:168
  25.6 4.4 %collective-permute-start.14 = (bf16[36,1440]{1,0:T(8,128)(2,1)S(1)}, bf16[36,1440]{1,0:T(8,128)(2,1)S(1)}, u32[]{:S(2)}, u32[]{:S(2)}) collective-permute-start(bf16[36,1440]{1,0:T(8,128)(2,1)S(1)} %collective-permute-done.5.rest_5_), channel_id=1, source_target_pairs={{0,2},{1,3},{2,0},{3,1},{4,6},{5,7},{6,4},{7,5},{8,10},{9,11},{10,... | collective-permute-start | bytes 311048 | tf_op jit(solution)/shard_map/ppermute | solution.py:168
  26.1 3.9 %collective-permute-start.12 = (bf16[36,1440]{1,0:T(8,128)(2,1)S(1)}, bf16[36,1440]{1,0:T(8,128)(2,1)S(1)}, u32[]{:S(2)}, u32[]{:S(2)}) collective-permute-start(bf16[36,1440]{1,0:T(8,128)(2,1)S(1)} %collective-permute-done.3.rest_3_), channel_id=1, source_target_pairs={{0,2},{1,3},{2,0},{3,1},{4,6},{5,7},{6,4},{7,5},{8,10},{9,11},{10,... | collective-permute-start | bytes 311048 | tf_op jit(solution)/shard_map/ppermute | solution.py:168
  35.0 21.5 %collective-permute-start.17 = (bf16[196,864]{1,0:T(8,128)(2,1)S(1)}, bf16[196,864]{1,0:T(8,128)(2,1)S(1)}, u32[]{:S(2)}, u32[]{:S(2)}) collective-permute-start(bf16[196,864]{1,0:T(8,128)(2,1)S(1)} %shard_map.108), channel_id=1, source_target_pairs={{0,1},{1,0},{2,3},{3,2},{4,5},{5,4},{6,7},{7,6},{8,9},{9,8},{10,11... | collective-permute-start | bytes 1016072 | tf_op jit(solution)/shard_map/ppermute | solution.py:168
  36.4 14.4 %collective-permute-start.19 = (bf16[2,36,864]{2,1,0:T(8,128)(2,1)S(1)}, bf16[2,36,864]{2,1,0:T(8,128)(2,1)S(1)}, u32[]{:S(2)}, u32[]{:S(2)}) collective-permute-start(bf16[2,36,864]{2,1,0:T(8,128)(2,1)S(1)} %get-tuple-element.56), channel_id=1, source_target_pairs={{0,4},{1,5},{2,6},{3,7},{4,0},{5,1},{6,2},{7,3},{8,12},{9,13},{10,... | collective-permute-start | bytes 373256 | tf_op jit(solution)/shard_map/ppermute | solution.py:168
  37.8 6.7 %collective-permute-start.21 = (bf16[36,864]{1,0:T(8,128)(2,1)S(1)}, bf16[36,864]{1,0:T(8,128)(2,1)S(1)}, u32[]{:S(2)}, u32[]{:S(2)}) collective-permute-start(bf16[36,864]{1,0:T(8,128)(2,1)S(1)} %get-tuple-element.59), channel_id=1, source_target_pairs={{0,4},{1,5},{2,6},{3,7},{4,0},{5,1},{6,2},{7,3},{8,12},{9,13},{10,... | collective-permute-start | bytes 186632 | tf_op jit(solution)/shard_map/ppermute | solution.py:168
  38.5 9.2 %collective-permute-start.23 = (bf16[36,864]{1,0:T(8,128)(2,1)S(1)}, bf16[36,864]{1,0:T(8,128)(2,1)S(1)}, u32[]{:S(2)}, u32[]{:S(2)}) collective-permute-start(bf16[36,864]{1,0:T(8,128)(2,1)S(1)} %get-tuple-element.60), channel_id=1, source_target_pairs={{0,4},{1,5},{2,6},{3,7},{4,0},{5,1},{6,2},{7,3},{8,12},{9,13},{10,... | collective-permute-start | bytes 186632 | tf_op jit(solution)/shard_map/ppermute | solution.py:168
  44.6 8.5 %collective-permute-start.22 = (bf16[36,864]{1,0:T(8,128)(2,1)S(1)}, bf16[36,864]{1,0:T(8,128)(2,1)S(1)}, u32[]{:S(2)}, u32[]{:S(2)}) collective-permute-start(bf16[36,864]{1,0:T(8,128)(2,1)S(1)} %shard_map.114), channel_id=1, source_target_pairs={{0,24},{1,25},{2,26},{3,27},{4,28},{5,29},{6,30},{7,31},{8,16},{9,... | collective-permute-start | bytes 186632 | tf_op jit(solution)/shard_map/ppermute | solution.py:168
  47.8 5.2 %collective-permute-start.24 = (bf16[36,288]{1,0:T(8,128)(2,1)S(1)}, bf16[36,288]{1,0:T(8,128)(2,1)S(1)}, u32[]{:S(2)}, u32[]{:S(2)}) collective-permute-start(bf16[36,288]{1,0:T(8,128)(2,1)S(1)} %get-tuple-element.61), channel_id=1, source_target_pairs={{0,16},{1,17},{2,18},{3,19},{4,20},{5,21},{6,22},{7,23},{8,24},{9,... | collective-permute-start | bytes 62216 | tf_op jit(solution)/shard_map/ppermute | solution.py:168
  48.3 9.6 %collective-permute-start.26 = (bf16[36,576]{1,0:T(8,128)(2,1)S(1)}, bf16[36,576]{1,0:T(8,128)(2,1)S(1)}, u32[]{:S(2)}, u32[]{:S(2)}) collective-permute-start(bf16[36,576]{1,0:T(8,128)(2,1)S(1)} %get-tuple-element.64), channel_id=1, source_target_pairs={{0,16},{1,17},{2,18},{3,19},{4,20},{5,21},{6,22},{7,23},{8,24},{9,... | collective-permute-start | bytes 124424 | tf_op jit(solution)/shard_map/ppermute | solution.py:168
  50.8 4.4 %collective-permute-start.20 = (bf16[36,864]{1,0:T(8,128)(2,1)S(1)}, bf16[36,864]{1,0:T(8,128)(2,1)S(1)}, u32[]{:S(2)}, u32[]{:S(2)}) collective-permute-start(bf16[36,864]{1,0:T(8,128)(2,1)S(1)} %get-tuple-element.58), channel_id=1, source_target_pairs={{0,8},{1,9},{2,10},{3,11},{4,12},{5,13},{6,14},{7,15},{8,0},{9,1},... | collective-permute-start | bytes 186632 | tf_op jit(solution)/shard_map/ppermute | solution.py:168
  55.4 4.0 %collective-permute-start.25 = (bf16[36,288]{1,0:T(8,128)(2,1)S(1)}, bf16[36,288]{1,0:T(8,128)(2,1)S(1)}, u32[]{:S(2)}, u32[]{:S(2)}) collective-permute-start(bf16[36,288]{1,0:T(8,128)(2,1)S(1)} %get-tuple-element.62), channel_id=1, source_target_pairs={{0,1},{1,0},{2,3},{3,2},{4,5},{5,4},{6,7},{7,6},{8,9},{9,8},{10,11... | collective-permute-start | bytes 62216 | tf_op jit(solution)/shard_map/ppermute | solution.py:168
  (9 other events, 25.6 us)

commit v3 on v2

--- a/solution.py
+++ b/solution.py
@@ -377,20 +377,21 @@
     send_ref[:, D:] = mixed_ref[FSLOT : FSLOT + FRAME_TOK, :]
 
 
-def late_kernel(low_ref, high_ref, dq_ref, e_ref, order_ref, nat_ref, oth_ref):
-    order = order_ref[...]
-    own = d_normed_of(0, low_ref, high_ref, dq_ref, e_ref).astype(BF16)
-    nat_ref[...] = dot(own, order, NT)[:FRAME_TOK].astype(BF16)
+def late_kernel(low_ref, high_ref, dq_ref, e_ref, own_ref):
+    own_ref[...] = d_normed_of(0, low_ref, high_ref, dq_ref, e_ref).astype(BF16)
+
+
+def last_kernel(
+    yone_ref, second_ref, dtwo_ref, gain_ref, got_ref, own_ref, mixed_ref, outh_ref, low_ref, high_ref, order_ref, x_ref, dx_ref
+):
     other = 1 - lax.axis_index("seq")
     select = order_ref[pl.ds(pl.multiple_of(other * HALF, HALF), HALF), :]
-    oth_ref[...] = (dot(select[:, :LOW], low_ref[:, QKV:]) + dot(select[:, LOW:], high_ref[:, QKV:])).astype(BF16)
-
-
-def last_kernel(yone_ref, second_ref, dtwo_ref, gain_ref, got_ref, dn_ref, mixed_ref, outh_ref, oth_ref, x_ref, dx_ref):
-    branch = dot(mixed_ref[:FRAME_TOK, :], outh_ref[...]) + dot(got_ref[:, D:], oth_ref[...])
+    out_other = (dot(select[:, :LOW], low_ref[:, QKV:]) + dot(select[:, LOW:], high_ref[:, QKV:])).astype(BF16)
+    own = dot(own_ref[...], order_ref[...], NT)[:FRAME_TOK]
+    branch = dot(mixed_ref[:FRAME_TOK, :], outh_ref[...]) + dot(got_ref[:, D:], out_other)
     x_ref[...] = (yone_ref[...].astype(F32) - branch).astype(BF16)
     xhat, inverse = standardize(second_ref[...].astype(F32))
-    gained = (dn_ref[...].astype(F32) + got_ref[:, :D].astype(F32)) * gain_ref[...].reshape(1, D)
+    gained = (own + got_ref[:, :D].astype(F32)) * gain_ref[...].reshape(1, D)
     lower = inverse * (
         gained
         - jnp.mean(gained, axis=-1, keepdims=True)
@@ -605,17 +606,17 @@
         moved=4_000_000,
     )
     got = swap(send, OVER_Y)
-    d_normed, out_oth = call(
+    d_normed = call(
         late_kernel,
-        (shape(FRAME_TOK, D), shape(HALF, D)),
-        (w_low, w_high, d_q, e, order),
+        shape(FSLOT, REL),
+        (w_low, w_high, d_q, e),
         flops=1_000_000_000,
         moved=3_000_000,
     )
     x_one, dx_two = call(
         last_kernel,
         (shape(FRAME_TOK, D), shape(FRAME_TOK, D)),
-        (y_one[0], second_here, d_two[0], gain_here, got, d_normed, mixed, out_own, out_oth),
+        (y_one[0], second_here, d_two[0], gain_here, got, d_normed, mixed, out_own, w_low, w_high, order),
         flops=300_000_000,
         moved=3_000_000,
     )

time: 60.3 us -> 60.3 us (level)
  no operation moved by 1% of the time
where the time goes in v3:
time: 60.3 us; the launch traced here: 60.1 us
  starting transfers between devices  28.3 us (47%)
  Pallas kernels  14.5 us (24%)
  waiting for transfers between devices  14.1 us (23%)
  local copies, waits for them, and re-layouts  1.77 us (3%)
  between operations  1.51 us (3%)
    ppermute x27, starting transfers between devices, swap(): return lax.ppermute(array, AXES, [(i, i ^ mask) for i in range(32)])  28.3 us
    pallas_call x15, Pallas kernels, call(): pl.pallas_call(kernel, out_shape=outs, in_specs=[pl.BlockSpec(memory_spac...  14.5 us
    ppermute x27, waiting for transfers between devices, swap(): return lax.ppermute(array, AXES, [(i, i ^ mask) for i in range(32)])  14.1 us
    unnamed x12, local copies, waits for them, and re-layouts  1.65 us
  transfers between devices with their start and end apart: 27, of which 8 were waited for; matrix products, arithmetic and copies ran while one was open for 0% of the time, Pallas kernels for 14%

profile of v3, /device:TPU:0, one launch (start us, length us, event | category | flops | bytes accessed | tf_op | source)
XLA Modules:
  0.0 60.1 jit_solution(570283361016649789)
XLA Ops:
  0.6 1.7 %shard_map.105.rest_0_ = bf16[36,1440]{1,0:T(8,128)(2,1)} custom-call(bf16[36,1728]{1,0:T(8,128)(2,1)} %qkv_hbm.1, bf16[36,576]{1,0:T(8,128)(2,1)} %out_hbm.1), custom_call_target="tpu_custom_call" | custom-call | bytes 400000 | tf_op jit(solution)/shard_map/pallas_call | solution.py:474
  2.4 4.1 %collective-permute-start.4 = (bf16[36,1440]{1,0:T(8,128)(2,1)}, bf16[36,1440]{1,0:T(8,128)(2,1)S(1)}, u32[]{:S(2)}, u32[]{:S(2)}) collective-permute-start(bf16[36,1440]{1,0:T(8,128)(2,1)} %shard_map.105.rest_0_), channel_id=1, source_target_pairs={{0,16},{1,17},{2,18},{3,19},{4,20},{5,21},{6,22},{7,23},{8,24},{9,... | collective-permute-start | bytes 311048 | tf_op jit(solution)/shard_map/ppermute | solution.py:168
  6.5 1.6 %collective-permute-start.2 = (bf16[36,1440]{1,0:T(8,128)(2,1)}, bf16[36,1440]{1,0:T(8,128)(2,1)S(1)}, u32[]{:S(2)}, u32[]{:S(2)}) collective-permute-start(bf16[36,1440]{1,0:T(8,128)(2,1)} %shard_map.105.rest_0_), channel_id=1, source_target_pairs={{0,8},{1,9},{2,10},{3,11},{4,12},{5,13},{6,14},{7,15},{8,0},{9,1},... | collective-permute-start | bytes 311048 | tf_op jit(solution)/shard_map/ppermute | solution.py:168
  8.1 1.5 %collective-permute-start.1 = (bf16[36,1440]{1,0:T(8,128)(2,1)}, bf16[36,1440]{1,0:T(8,128)(2,1)S(1)}, u32[]{:S(2)}, u32[]{:S(2)}) collective-permute-start(bf16[36,1440]{1,0:T(8,128)(2,1)} %shard_map.105.rest_0_), channel_id=1, source_target_pairs={{0,4},{1,5},{2,6},{3,7},{4,0},{5,1},{6,2},{7,3},{8,12},{9,13},{10,... | collective-permute-start | bytes 311048 | tf_op jit(solution)/shard_map/ppermute | solution.py:168
  9.6 1.5 %collective-permute-start = (bf16[196,576]{1,0:T(8,128)(2,1)}, bf16[196,576]{1,0:T(8,128)(2,1)S(1)}, u32[]{:S(2)}, u32[]{:S(2)}) collective-permute-start(bf16[196,576]{1,0:T(8,128)(2,1)} %bitcast.8), channel_id=1, source_target_pairs={{0,1},{1,0},{2,3},{3,2},{4,5},{5,4},{6,7},{7,6},{8,9},{9,8},{10,11... | collective-permute-start | bytes 677384 | tf_op jit(solution)/shard_map/ppermute | solution.py:168
  11.1 1.7 %collective-permute-done.4.rest_4_ = bf16[36,1440]{1,0:T(8,128)(2,1)S(1)} collective-permute-done((bf16[36,1440]{1,0:T(8,128)(2,1)}, bf16[36,1440]{1,0:T(8,128)(2,1)S(1)}, u32[]{:S(2)}, u32[]{:S(2)}) %collective-permute-start.4) | collective-permute-done | bytes 103712 | tf_op jit(solution)/shard_map/ppermute | solution.py:168
  13.9 1.5 %collective-permute-start.5 = (bf16[36,1440]{1,0:T(8,128)(2,1)S(1)}, bf16[36,1440]{1,0:T(8,128)(2,1)S(1)}, u32[]{:S(2)}, u32[]{:S(2)}) collective-permute-start(bf16[36,1440]{1,0:T(8,128)(2,1)S(1)} %collective-permute-done.4.rest_4_), channel_id=1, source_target_pairs={{0,4},{1,5},{2,6},{3,7},{4,0},{5,1},{6,2},{7,3},{8,12},{9,13},{10,... | collective-permute-start | bytes 311048 | tf_op jit(solution)/shard_map/ppermute | solution.py:168
  16.0 2.5 %collective-permute-done.6.rest_6_ = bf16[36,1440]{1,0:T(8,128)(2,1)S(1)} collective-permute-done((bf16[36,1440]{1,0:T(8,128)(2,1)S(1)}, bf16[36,1440]{1,0:T(8,128)(2,1)S(1)}, u32[]{:S(2)}, u32[]{:S(2)}) %collective-permute-start.6) | collective-permute-done | bytes 103712 | tf_op jit(solution)/shard_map/ppermute | solution.py:168
  18.5 0.9 %collective-permute-done.5.rest_5_ = bf16[36,1440]{1,0:T(8,128)(2,1)S(1)} collective-permute-done((bf16[36,1440]{1,0:T(8,128)(2,1)S(1)}, bf16[36,1440]{1,0:T(8,128)(2,1)S(1)}, u32[]{:S(2)}, u32[]{:S(2)}) %collective-permute-start.5) | collective-permute-done | bytes 103712 | tf_op jit(solution)/shard_map/ppermute | solution.py:168
  19.4 2.2 %collective-permute-start.7 = (bf16[36,1440]{1,0:T(8,128)(2,1)S(1)}, bf16[36,1440]{1,0:T(8,128)(2,1)S(1)}, u32[]{:S(2)}, u32[]{:S(2)}) collective-permute-start(bf16[36,1440]{1,0:T(8,128)(2,1)S(1)} %collective-permute-done.6.rest_6_), channel_id=1, source_target_pairs={{0,4},{1,5},{2,6},{3,7},{4,0},{5,1},{6,2},{7,3},{8,12},{9,13},{10,... | collective-permute-start | bytes 311048 | tf_op jit(solution)/shard_map/ppermute | solution.py:168
  21.7 1.5 %collective-permute-start.11 = (bf16[196,576]{1,0:T(8,128)(2,1)}, bf16[196,576]{1,0:T(8,128)(2,1)S(1)}, u32[]{:S(2)}, u32[]{:S(2)}) collective-permute-start(bf16[196,576]{1,0:T(8,128)(2,1)} %bitcast.10), channel_id=1, source_target_pairs={{0,1},{1,0},{2,3},{3,2},{4,5},{5,4},{6,7},{7,6},{8,9},{9,8},{10,11... | collective-permute-start | bytes 677384 | tf_op jit(solution)/shard_map/ppermute | solution.py:168
  23.9 0.9 %copy-done.3 = bf16[1,196,576]{2,1,0:T(8,128)(2,1)S(1)} copy-done((bf16[1,196,576]{2,1,0:T(8,128)(2,1)S(1)}, bf16[1,196,576]{2,1,0:T(8,128)(2,1)}, u32[]{:S(2)}) %copy-start.3) | copy-done | bytes 225816
  26.6 2.4 %shard_map.104 = (bf16[416,768]{1,0:T(8,128)(2,1)S(1)}, bf16[2,768,208]{2,1,0:T(8,128)(2,1)S(1)}, bf16[256,768]{1,0:T(8,128)(2,1)S(1)}, bf16[768,256]{1,0:T(8,128)(2,1)S(1)}, bf16[576,768]{1,0:T(8,128)(2,1)S(1)}) custom-call(bf16[196,576]{1,0:T(8,128)(2,1)S(1)} %get-tuple-element.32.own_ref.second_ref, bf16[196,576]{1,0:T(8,128)(2,1)S(1)} %collective-permute-done.peer_ref, ...), custom_call_target="tpu_custom_call" | custom-call | flops 1200000000 | bytes 3000000 | tf_op jit(solution)/shard_map/pallas_call | solution.py:474
  29.1 0.9 %shard_map.106 = (bf16[512,1440]{1,0:T(8,128)(2,1)S(1)}, f32[416,288]{1,0:T(8,128)S(1)}, f32[256,608]{1,0:T(8,128)S(1)}, f32[288,576]{1,0:T(8,128)S(1)}) custom-call(bf16[416,768]{1,0:T(8,128)(2,1)S(1)} %get-tuple-element.34.rel_ref, bf16[256,768]{1,0:T(8,128)(2,1)S(1)} %get-tuple-element.35.pool_ref, bf16[576,768]{1,0:T(8,128)(2,1)S(1)} %get-tuple-element.36.order_ref, ...), custom_call_target="tpu_custom_call" | custom-call | flops 800000000 | bytes 4000000 | tf_op jit(solution)/shard_map/pallas_call | solution.py:474
  30.1 3.4 %shard_map.107 = (bf16[8,36,864]{2,1,0:T(8,128)(2,1)S(1)}, bf16[256,1440]{1,0:T(8,128)(2,1)S(1)}, bf16[416,384]{1,0:T(8,128)(2,1)S(1)}, bf16[256,608]{1,0:T(8,12...) custom-call(s32[1]{0:T(128)S(6)} %copy.13.valid_ref, ...), custom_call_target="tpu_custom_call" | custom-call | flops 4000000000 | bytes 8000000 | tf_op jit(solution)/shard_map/pallas_call | solution.py:474
  33.7 1.3 %shard_map.108 = bf16[196,864]{1,0:T(8,128)(2,1)S(1)} custom-call(bf16[512,1440]{1,0:T(8,128)(2,1)S(1)} %get-tuple-element.37.low_ref, bf16[256,1440]{1,0:T(8,128)(2,1)S(1)} %get-tuple-element.43.high_ref, bf16[416,384]{1,0:T(8,128)(2,1)S(1)} %get-tuple-element.44.dq_ref, bf16[256,608]{1,0:T(8,128)(2,1)S(1)} %get-tuple-element.45.e_ref, ...), custom_call_target="tpu_custom_call" | custom-call | flops 600000000 | bytes 4000000 | tf_op jit(solution)/shard_map/pallas_call | solution.py:474
  36.3 1.5 %collective-permute-start.19 = (bf16[2,36,864]{2,1,0:T(8,128)(2,1)S(1)}, bf16[2,36,864]{2,1,0:T(8,128)(2,1)S(1)}, u32[]{:S(2)}, u32[]{:S(2)}) collective-permute-start(bf16[2,36,864]{2,1,0:T(8,128)(2,1)S(1)} %get-tuple-element.52), channel_id=1, source_target_pairs={{0,4},{1,5},{2,6},{3,7},{4,0},{5,1},{6,2},{7,3},{8,12},{9,13},{10,... | collective-permute-start | bytes 373256 | tf_op jit(solution)/shard_map/ppermute | solution.py:168
  38.4 1.4 %collective-permute-start.23 = (bf16[36,864]{1,0:T(8,128)(2,1)S(1)}, bf16[36,864]{1,0:T(8,128)(2,1)S(1)}, u32[]{:S(2)}, u32[]{:S(2)}) collective-permute-start(bf16[36,864]{1,0:T(8,128)(2,1)S(1)} %get-tuple-element.56), channel_id=1, source_target_pairs={{0,4},{1,5},{2,6},{3,7},{4,0},{5,1},{6,2},{7,3},{8,12},{9,13},{10,... | collective-permute-start | bytes 186632 | tf_op jit(solution)/shard_map/ppermute | solution.py:168
  39.8 4.7 %collective-permute-done.21.got_ref = bf16[36,864]{1,0:T(8,128)(2,1)S(1)} collective-permute-done((bf16[36,864]{1,0:T(8,128)(2,1)S(1)}, bf16[36,864]{1,0:T(8,128)(2,1)S(1)}, u32[]{:S(2)}, u32[]{:S(2)}) %collective-permute-start.21) | collective-permute-done | bytes 62240 | tf_op jit(solution)/shard_map/ppermute | solution.py:168
  44.5 3.1 %collective-permute-start.22 = (bf16[36,864]{1,0:T(8,128)(2,1)S(1)}, bf16[36,864]{1,0:T(8,128)(2,1)S(1)}, u32[]{:S(2)}, u32[]{:S(2)}) collective-permute-start(bf16[36,864]{1,0:T(8,128)(2,1)S(1)} %shard_map.114), channel_id=1, source_target_pairs={{0,24},{1,25},{2,26},{3,27},{4,28},{5,29},{6,30},{7,31},{8,16},{9,... | collective-permute-start | bytes 186632 | tf_op jit(solution)/shard_map/ppermute | solution.py:168
  48.3 2.4 %collective-permute-start.26 = (bf16[36,576]{1,0:T(8,128)(2,1)S(1)}, bf16[36,576]{1,0:T(8,128)(2,1)S(1)}, u32[]{:S(2)}, u32[]{:S(2)}) collective-permute-start(bf16[36,576]{1,0:T(8,128)(2,1)S(1)} %get-tuple-element.60), channel_id=1, source_target_pairs={{0,16},{1,17},{2,18},{3,19},{4,20},{5,21},{6,22},{7,23},{8,24},{9,... | collective-permute-start | bytes 124424 | tf_op jit(solution)/shard_map/ppermute | solution.py:168
  53.0 2.2 %collective-permute-done.20.a_ref = bf16[36,864]{1,0:T(8,128)(2,1)S(1)} collective-permute-done((bf16[36,864]{1,0:T(8,128)(2,1)S(1)}, bf16[36,864]{1,0:T(8,128)(2,1)S(1)}, u32[]{:S(2)}, u32[]{:S(2)}) %collective-permute-start.20) | collective-permute-done | bytes 62240 | tf_op jit(solution)/shard_map/ppermute | solution.py:168
  55.4 1.1 %collective-permute-start.25 = (bf16[36,288]{1,0:T(8,128)(2,1)S(1)}, bf16[36,288]{1,0:T(8,128)(2,1)S(1)}, u32[]{:S(2)}, u32[]{:S(2)}) collective-permute-start(bf16[36,288]{1,0:T(8,128)(2,1)S(1)} %get-tuple-element.58), channel_id=1, source_target_pairs={{0,1},{1,0},{2,3},{3,2},{4,5},{5,4},{6,7},{7,6},{8,9},{9,8},{10,11... | collective-permute-start | bytes 62216 | tf_op jit(solution)/shard_map/ppermute | solution.py:168
  56.5 2.1 %shard_map.110 = (bf16[196,576]{1,0:T(8,128)(2,1)}, bf16[196,576]{1,0:T(8,128)(2,1)}) custom-call(bf16[196,576]{1,0:T(8,128)(2,1)S(1)} %bitcast.6, bf16[196,576]{1,0:T(8,128)(2,1)S(1)} %get-tuple-element.32.own_ref.second_ref, bf16[196,576]{1,0:T(8,128)(2,1)S(1)} %bitcast.7, f32[576]{0:T(1024)S(1)} %get-tuple-element.33.gain_ref, ...), custom_call_target="tpu_custom_call" | custom-call | flops 300000000 | bytes 3000000 | tf_op jit(solution)/shard_map/pallas_call | solution.py:474
  (59 shorter events, 10.3 us)
Async XLA Ops:
  2.4 10.4 %collective-permute-start.4 = (bf16[36,1440]{1,0:T(8,128)(2,1)}, bf16[36,1440]{1,0:T(8,128)(2,1)S(1)}, u32[]{:S(2)}, u32[]{:S(2)}) collective-permute-start(bf16[36,1440]{1,0:T(8,128)(2,1)} %shard_map.105.rest_0_), channel_id=1, source_target_pairs={{0,16},{1,17},{2,18},{3,19},{4,20},{5,21},{6,22},{7,23},{8,24},{9,... | collective-permute-start | bytes 311048 | tf_op jit(solution)/shard_map/ppermute | solution.py:168
  6.5 6.3 %collective-permute-start.8 = (bf16[36,1440]{1,0:T(8,128)(2,1)}, bf16[36,1440]{1,0:T(8,128)(2,1)S(1)}, u32[]{:S(2)}, u32[]{:S(2)}) collective-permute-start(bf16[36,1440]{1,0:T(8,128)(2,1)} %shard_map.105.rest_0_), channel_id=1, source_target_pairs={{0,2},{1,3},{2,0},{3,1},{4,6},{5,7},{6,4},{7,5},{8,10},{9,11},{10,... | collective-permute-start | bytes 311048 | tf_op jit(solution)/shard_map/ppermute | solution.py:168
  6.5 7.4 %collective-permute-start.2 = (bf16[36,1440]{1,0:T(8,128)(2,1)}, bf16[36,1440]{1,0:T(8,128)(2,1)S(1)}, u32[]{:S(2)}, u32[]{:S(2)}) collective-permute-start(bf16[36,1440]{1,0:T(8,128)(2,1)} %shard_map.105.rest_0_), channel_id=1, source_target_pairs={{0,8},{1,9},{2,10},{3,11},{4,12},{5,13},{6,14},{7,15},{8,0},{9,1},... | collective-permute-start | bytes 311048 | tf_op jit(solution)/shard_map/ppermute | solution.py:168
  8.1 7.4 %collective-permute-start.1 = (bf16[36,1440]{1,0:T(8,128)(2,1)}, bf16[36,1440]{1,0:T(8,128)(2,1)S(1)}, u32[]{:S(2)}, u32[]{:S(2)}) collective-permute-start(bf16[36,1440]{1,0:T(8,128)(2,1)} %shard_map.105.rest_0_), channel_id=1, source_target_pairs={{0,4},{1,5},{2,6},{3,7},{4,0},{5,1},{6,2},{7,3},{8,12},{9,13},{10,... | collective-permute-start | bytes 311048 | tf_op jit(solution)/shard_map/ppermute | solution.py:168
  9.6 16.5 %collective-permute-start = (bf16[196,576]{1,0:T(8,128)(2,1)}, bf16[196,576]{1,0:T(8,128)(2,1)S(1)}, u32[]{:S(2)}, u32[]{:S(2)}) collective-permute-start(bf16[196,576]{1,0:T(8,128)(2,1)} %bitcast.8), channel_id=1, source_target_pairs={{0,1},{1,0},{2,3},{3,2},{4,5},{5,4},{6,7},{7,6},{8,9},{9,8},{10,11... | collective-permute-start | bytes 677384 | tf_op jit(solution)/shard_map/ppermute | solution.py:168
  12.8 5.7 %collective-permute-start.6 = (bf16[36,1440]{1,0:T(8,128)(2,1)S(1)}, bf16[36,1440]{1,0:T(8,128)(2,1)S(1)}, u32[]{:S(2)}, u32[]{:S(2)}) collective-permute-start(bf16[36,1440]{1,0:T(8,128)(2,1)S(1)} %collective-permute-done.4.rest_4_), channel_id=1, source_target_pairs={{0,8},{1,9},{2,10},{3,11},{4,12},{5,13},{6,14},{7,15},{8,0},{9,1},... | collective-permute-start | bytes 311048 | tf_op jit(solution)/shard_map/ppermute | solution.py:168
  13.9 5.5 %collective-permute-start.5 = (bf16[36,1440]{1,0:T(8,128)(2,1)S(1)}, bf16[36,1440]{1,0:T(8,128)(2,1)S(1)}, u32[]{:S(2)}, u32[]{:S(2)}) collective-permute-start(bf16[36,1440]{1,0:T(8,128)(2,1)S(1)} %collective-permute-done.4.rest_4_), channel_id=1, source_target_pairs={{0,4},{1,5},{2,6},{3,7},{4,0},{5,1},{6,2},{7,3},{8,12},{9,13},{10,... | collective-permute-start | bytes 311048 | tf_op jit(solution)/shard_map/ppermute | solution.py:168
  15.5 6.2 %collective-permute-start.10 = (bf16[36,1440]{1,0:T(8,128)(2,1)S(1)}, bf16[36,1440]{1,0:T(8,128)(2,1)S(1)}, u32[]{:S(2)}, u32[]{:S(2)}) collective-permute-start(bf16[36,1440]{1,0:T(8,128)(2,1)S(1)} %collective-permute-done.2.rest_2_), channel_id=1, source_target_pairs={{0,2},{1,3},{2,0},{3,1},{4,6},{5,7},{6,4},{7,5},{8,10},{9,11},{10,... | collective-permute-start | bytes 311048 | tf_op jit(solution)/shard_map/ppermute | solution.py:168
  15.5 10.0 %collective-permute-start.3 = (bf16[36,1440]{1,0:T(8,128)(2,1)S(1)}, bf16[36,1440]{1,0:T(8,128)(2,1)S(1)}, u32[]{:S(2)}, u32[]{:S(2)}) collective-permute-start(bf16[36,1440]{1,0:T(8,128)(2,1)S(1)} %collective-permute-done.2.rest_2_), channel_id=1, source_target_pairs={{0,4},{1,5},{2,6},{3,7},{4,0},{5,1},{6,2},{7,3},{8,12},{9,13},{10,... | collective-permute-start | bytes 311048 | tf_op jit(solution)/shard_map/ppermute | solution.py:168
  18.5 7.1 %collective-permute-start.9 = (bf16[36,1440]{1,0:T(8,128)(2,1)S(1)}, bf16[36,1440]{1,0:T(8,128)(2,1)S(1)}, u32[]{:S(2)}, u32[]{:S(2)}) collective-permute-start(bf16[36,1440]{1,0:T(8,128)(2,1)S(1)} %collective-permute-done.1.rest_1_), channel_id=1, source_target_pairs={{0,2},{1,3},{2,0},{3,1},{4,6},{5,7},{6,4},{7,5},{8,10},{9,11},{10,... | collective-permute-start | bytes 311048 | tf_op jit(solution)/shard_map/ppermute | solution.py:168
  19.4 6.8 %collective-permute-start.7 = (bf16[36,1440]{1,0:T(8,128)(2,1)S(1)}, bf16[36,1440]{1,0:T(8,128)(2,1)S(1)}, u32[]{:S(2)}, u32[]{:S(2)}) collective-permute-start(bf16[36,1440]{1,0:T(8,128)(2,1)S(1)} %collective-permute-done.6.rest_6_), channel_id=1, source_target_pairs={{0,4},{1,5},{2,6},{3,7},{4,0},{5,1},{6,2},{7,3},{8,12},{9,13},{10,... | collective-permute-start | bytes 311048 | tf_op jit(solution)/shard_map/ppermute | solution.py:168
  21.7 8.3 %collective-permute-start.11 = (bf16[196,576]{1,0:T(8,128)(2,1)}, bf16[196,576]{1,0:T(8,128)(2,1)S(1)}, u32[]{:S(2)}, u32[]{:S(2)}) collective-permute-start(bf16[196,576]{1,0:T(8,128)(2,1)} %bitcast.10), channel_id=1, source_target_pairs={{0,1},{1,0},{2,3},{3,2},{4,5},{5,4},{6,7},{7,6},{8,9},{9,8},{10,11... | collective-permute-start | bytes 677384 | tf_op jit(solution)/shard_map/ppermute | solution.py:168
  25.5 4.5 %collective-permute-start.15 = (bf16[36,1440]{1,0:T(8,128)(2,1)S(1)}, bf16[36,1440]{1,0:T(8,128)(2,1)S(1)}, u32[]{:S(2)}, u32[]{:S(2)}) collective-permute-start(bf16[36,1440]{1,0:T(8,128)(2,1)S(1)} %collective-permute-done.6.rest_6_), channel_id=1, source_target_pairs={{0,2},{1,3},{2,0},{3,1},{4,6},{5,7},{6,4},{7,5},{8,10},{9,11},{10,... | collective-permute-start | bytes 311048 | tf_op jit(solution)/shard_map/ppermute | solution.py:168
  25.6 4.4 %collective-permute-start.14 = (bf16[36,1440]{1,0:T(8,128)(2,1)S(1)}, bf16[36,1440]{1,0:T(8,128)(2,1)S(1)}, u32[]{:S(2)}, u32[]{:S(2)}) collective-permute-start(bf16[36,1440]{1,0:T(8,128)(2,1)S(1)} %collective-permute-done.5.rest_5_), channel_id=1, source_target_pairs={{0,2},{1,3},{2,0},{3,1},{4,6},{5,7},{6,4},{7,5},{8,10},{9,11},{10,... | collective-permute-start | bytes 311048 | tf_op jit(solution)/shard_map/ppermute | solution.py:168
  26.1 3.9 %collective-permute-start.12 = (bf16[36,1440]{1,0:T(8,128)(2,1)S(1)}, bf16[36,1440]{1,0:T(8,128)(2,1)S(1)}, u32[]{:S(2)}, u32[]{:S(2)}) collective-permute-start(bf16[36,1440]{1,0:T(8,128)(2,1)S(1)} %collective-permute-done.3.rest_3_), channel_id=1, source_target_pairs={{0,2},{1,3},{2,0},{3,1},{4,6},{5,7},{6,4},{7,5},{8,10},{9,11},{10,... | collective-permute-start | bytes 311048 | tf_op jit(solution)/shard_map/ppermute | solution.py:168
  35.0 21.5 %collective-permute-start.17 = (bf16[196,864]{1,0:T(8,128)(2,1)S(1)}, bf16[196,864]{1,0:T(8,128)(2,1)S(1)}, u32[]{:S(2)}, u32[]{:S(2)}) collective-permute-start(bf16[196,864]{1,0:T(8,128)(2,1)S(1)} %shard_map.108), channel_id=1, source_target_pairs={{0,1},{1,0},{2,3},{3,2},{4,5},{5,4},{6,7},{7,6},{8,9},{9,8},{10,11... | collective-permute-start | bytes 1016072 | tf_op jit(solution)/shard_map/ppermute | solution.py:168
  36.3 14.4 %collective-permute-start.19 = (bf16[2,36,864]{2,1,0:T(8,128)(2,1)S(1)}, bf16[2,36,864]{2,1,0:T(8,128)(2,1)S(1)}, u32[]{:S(2)}, u32[]{:S(2)}) collective-permute-start(bf16[2,36,864]{2,1,0:T(8,128)(2,1)S(1)} %get-tuple-element.52), channel_id=1, source_target_pairs={{0,4},{1,5},{2,6},{3,7},{4,0},{5,1},{6,2},{7,3},{8,12},{9,13},{10,... | collective-permute-start | bytes 373256 | tf_op jit(solution)/shard_map/ppermute | solution.py:168
  37.8 6.7 %collective-permute-start.21 = (bf16[36,864]{1,0:T(8,128)(2,1)S(1)}, bf16[36,864]{1,0:T(8,128)(2,1)S(1)}, u32[]{:S(2)}, u32[]{:S(2)}) collective-permute-start(bf16[36,864]{1,0:T(8,128)(2,1)S(1)} %get-tuple-element.55), channel_id=1, source_target_pairs={{0,4},{1,5},{2,6},{3,7},{4,0},{5,1},{6,2},{7,3},{8,12},{9,13},{10,... | collective-permute-start | bytes 186632 | tf_op jit(solution)/shard_map/ppermute | solution.py:168
  38.4 9.2 %collective-permute-start.23 = (bf16[36,864]{1,0:T(8,128)(2,1)S(1)}, bf16[36,864]{1,0:T(8,128)(2,1)S(1)}, u32[]{:S(2)}, u32[]{:S(2)}) collective-permute-start(bf16[36,864]{1,0:T(8,128)(2,1)S(1)} %get-tuple-element.56), channel_id=1, source_target_pairs={{0,4},{1,5},{2,6},{3,7},{4,0},{5,1},{6,2},{7,3},{8,12},{9,13},{10,... | collective-permute-start | bytes 186632 | tf_op jit(solution)/shard_map/ppermute | solution.py:168
  44.5 8.5 %collective-permute-start.22 = (bf16[36,864]{1,0:T(8,128)(2,1)S(1)}, bf16[36,864]{1,0:T(8,128)(2,1)S(1)}, u32[]{:S(2)}, u32[]{:S(2)}) collective-permute-start(bf16[36,864]{1,0:T(8,128)(2,1)S(1)} %shard_map.114), channel_id=1, source_target_pairs={{0,24},{1,25},{2,26},{3,27},{4,28},{5,29},{6,30},{7,31},{8,16},{9,... | collective-permute-start | bytes 186632 | tf_op jit(solution)/shard_map/ppermute | solution.py:168
  47.8 5.2 %collective-permute-start.24 = (bf16[36,288]{1,0:T(8,128)(2,1)S(1)}, bf16[36,288]{1,0:T(8,128)(2,1)S(1)}, u32[]{:S(2)}, u32[]{:S(2)}) collective-permute-start(bf16[36,288]{1,0:T(8,128)(2,1)S(1)} %get-tuple-element.57), channel_id=1, source_target_pairs={{0,16},{1,17},{2,18},{3,19},{4,20},{5,21},{6,22},{7,23},{8,24},{9,... | collective-permute-start | bytes 62216 | tf_op jit(solution)/shard_map/ppermute | solution.py:168
  48.3 10.3 %collective-permute-start.26 = (bf16[36,576]{1,0:T(8,128)(2,1)S(1)}, bf16[36,576]{1,0:T(8,128)(2,1)S(1)}, u32[]{:S(2)}, u32[]{:S(2)}) collective-permute-start(bf16[36,576]{1,0:T(8,128)(2,1)S(1)} %get-tuple-element.60), channel_id=1, source_target_pairs={{0,16},{1,17},{2,18},{3,19},{4,20},{5,21},{6,22},{7,23},{8,24},{9,... | collective-permute-start | bytes 124424 | tf_op jit(solution)/shard_map/ppermute | solution.py:168
  50.8 4.4 %collective-permute-start.20 = (bf16[36,864]{1,0:T(8,128)(2,1)S(1)}, bf16[36,864]{1,0:T(8,128)(2,1)S(1)}, u32[]{:S(2)}, u32[]{:S(2)}) collective-permute-start(bf16[36,864]{1,0:T(8,128)(2,1)S(1)} %get-tuple-element.54), channel_id=1, source_target_pairs={{0,8},{1,9},{2,10},{3,11},{4,12},{5,13},{6,14},{7,15},{8,0},{9,1},... | collective-permute-start | bytes 186632 | tf_op jit(solution)/shard_map/ppermute | solution.py:168
  55.4 4.0 %collective-permute-start.25 = (bf16[36,288]{1,0:T(8,128)(2,1)S(1)}, bf16[36,288]{1,0:T(8,128)(2,1)S(1)}, u32[]{:S(2)}, u32[]{:S(2)}) collective-permute-start(bf16[36,288]{1,0:T(8,128)(2,1)S(1)} %get-tuple-element.58), channel_id=1, source_target_pairs={{0,1},{1,0},{2,3},{3,2},{4,5},{5,4},{6,7},{7,6},{8,9},{9,8},{10,11... | collective-permute-start | bytes 62216 | tf_op jit(solution)/shard_map/ppermute | solution.py:168
  (9 other events, 25.6 us)
